TPU v7x, 256 devices: a whole 4x4x8 slice. The times are simulated.
256 devices in a mesh: gx: 4 (over x), gy: 8 (over z), gz: 8 (over y, core).
Axes of the slice: x: 4, y: 4, z: 8, core: 2. Of those that a mesh axis runs over, the one named last changes fastest.
Arguments:
- solution_old: float32 [1024, 32, 1024], P(('gx', 'gy', 'gz')), may hold values from -6 to 6
- right_side: float32 [1024, 32, 1024], P(('gx', 'gy', 'gz')), may hold values from -6 to 6
- acoef: float32 [1024, 32, 1024], P(('gx', 'gy', 'gz')), may hold values from 0.05 to 1
- bcoef: float32 [1024, 32, 1024], P(('gx', 'gy', 'gz')), may hold values from 0.25 to 4
- corners: int32 [3, 1024], replicated, may hold values from 0 to 992, as said below
Outputs:
- solution: float32 [128, 256, 1024], P('gx', 'gy', 'gz')
- residual: float32 [128, 256, 1024], P('gx', 'gy', 'gz')
Inputs may be any that keep to these rules, and one draw needn't show every extreme that they name: `corners`: each corner is a multiple of 32 in every dimension and the boxes tile the level one to one. The new owner of a box, the device whose block of 32 x 32 x 128 cells holds its corner, has the same gx and gz indices as the device that holds its row. At most one box moves from one device to any other device, and at most min(3, 7) boxes leave or reach one device; in each group of devices with one gx and one gz index, one device swaps a box with each of that many others, and every other device of the group passes one box on along a cycle through them.
All inputs are finite; a program needn't handle non-finite values.
Results may differ from a plain program's by a relative error of at most 0.00002.
Values sent between devices are 32-bit elements; how exact they have to be, the bound alone decides.
No kernel may reach another device: no remote copies, remote signals or barrier semaphores. Data moves between devices by JAX's collectives and lax.ppermute only.
A program may use at most 64 MiB of HBM per device.

v0:
```python
import functools
import itertools

import jax
import jax.numpy as jnp
from jax import lax
from jax.experimental import pallas as pl
from jax.experimental.pallas import tpu as pltpu
from jax.sharding import PartitionSpec as P

BOX = 32
N_GX, N_GY, N_GZ = 4, 8, 8
PER_DEV = 4
ROUNDS = 3
HALF = BOX // 2
SIDE = 3
PAIRS = HALF + 2 * SIDE
SENT = PAIRS - 2
SWEEPS = 2
F32 = jnp.float32
MIB = 1024 * 1024


def _colourings():
    table = {}
    for p1, p2 in itertools.combinations(range(1, 7), 2):
        codes = set()
        for cyc in itertools.product(range(3), repeat=7):
            if any(cyc[p] == cyc[p - 1] for p in range(7)):
                continue
            if [3 - cyc[p] - cyc[p - 1] for p in (0, p1, p2)] == [0, 1, 2]:
                codes.add(sum(c << (2 * i) for i, c in enumerate(list(cyc) + [0, 1, 2])))
        codes = sorted(codes)
        table[p1 * 7 + p2] = [codes[i % len(codes)] for i in range(CHOICES)]
    return table


CHOICES = 4
COLOURINGS = _colourings()
ORDERS = [sum(c << (2 * i) for i, c in enumerate(o)) for o in itertools.permutations(range(3))]


def _pick(flag, yes, no):
    return jnp.where(flag, jnp.int32(yes) if isinstance(yes, int) else yes, jnp.int32(no) if isinstance(no, int) else no)


def _chain(index, values):
    out = values[-1]
    for i in reversed(range(len(values) - 1)):
        out = jnp.where(index == i, values[i], out)
    return out


def _colour(code, edge):
    return lax.shift_right_logical(code, 2 * edge) & 3


def plan_kernel(
    table, f0, f1, f2, f3, plan, pay0, pay1, pay2, corners, own, succ, swap, spot, ubox, rows8, sems, sem
):
    whole = pltpu.make_async_copy(table, corners, sem)
    whole.start()
    whole.wait()
    gx, me, gz = lax.axis_index("gx"), lax.axis_index("gy"), lax.axis_index("gz")
    stride = N_GZ * PER_DEV
    bases = [gx * (N_GY * stride) + ((gz & 6) + c) * PER_DEV for c in range(2)]

    groups = []
    for c, base in enumerate(bases):
        hot = jnp.int32(0)
        rows = []
        for g in range(N_GY):
            row = [lax.shift_right_logical(corners[1, base + g * stride + s], 5) for s in range(PER_DEV)]
            rows.append(row)
            leaving = sum(_pick(o != g, 1, 0) for o in row)
            hot = hot + _pick(leaving == 3, g, 0)
            for s in range(PER_DEV):
                own[c * 32 + g * PER_DEV + s] = row[s]
        first = jnp.int32(0)
        for g in reversed(range(N_GY)):
            to_hot = jnp.int32(0)
            nxt = jnp.int32(0)
            for o in rows[g]:
                to_hot = to_hot + _pick(o == hot, 1, 0)
                nxt = nxt + _pick((o != g) & (o != hot), o, 0)
            is_swap = _pick(hot == g, 0, to_hot)
            succ[c * 8 + g] = nxt
            swap[c * 8 + g] = is_swap
            first = _pick(is_swap == 1, g, first)
        v = first
        p1 = jnp.int32(0)
        p2 = jnp.int32(0)
        mine = jnp.int32(-1)
        pred = jnp.int32(0)
        cycle = []
        for p in range(7):
            spot[c * 8 + p] = v
            cycle.append(v)
            if p:
                sw = swap[c * 8 + v] == 1
                p2 = _pick(sw & (p1 != 0), p, p2)
                p1 = _pick(sw & (p1 == 0), p, p1)
            mine = _pick(v == me, p, mine)
            nxt = succ[c * 8 + v]
            pred = _pick(nxt == me, v, pred)
            v = nxt
        key = p1 * 7 + p2
        codes = [jnp.int32(0)] * CHOICES
        for k, options in COLOURINGS.items():
            codes = [_pick(key == k, o, code) for o, code in zip(options, codes)]
        swaps = [cycle[0], spot[c * 8 + p1], spot[c * 8 + p2]]
        groups.append((hot, cycle, swaps, codes, mine, pred, p1))

    link, lane = iota(0), iota(1)
    order = _chain(lane & 7, ORDERS + ORDERS[:2])
    load = [jnp.zeros((8, 128), jnp.int32) for _ in range(2)]
    for c in range(2):
        hot, cycle, swaps, codes = groups[c][:4]
        code = _chain(lax.shift_right_logical(lane, 5 - 2 * c) & 3, codes)
        for e in range(10):
            colour = _colour(code, e)
            if c:
                colour = lax.shift_right_logical(order, 2 * colour) & 3
            unit = lax.shift_left(jnp.ones((8, 128), jnp.int32), 8 * colour)
            flows = [(cycle[e], cycle[(e + 1) % 7])] if e < 7 else [(hot, swaps[e - 7]), (swaps[e - 7], hot)]
            for i, j in flows:
                d = (j - i) & 7
                ahead = _pick(d <= 4, d, 0)
                back = _pick(d <= 4, 0, 8 - d)
                load[0] = load[0] + jnp.where(((link - i) & 7) < ahead, unit, 0)
                load[1] = load[1] + jnp.where(((i - link) & 7) < back, unit, 0)
    cost = jnp.zeros((8, 128), F32)
    for r in range(ROUNDS):
        busiest = jnp.maximum(*[(lax.shift_right_logical(v, 8 * r) & 255).astype(F32) for v in load])
        for shift in (4, 2, 1):
            busiest = jnp.maximum(busiest, sroll(busiest, shift))
        cost = cost + busiest
    best = jnp.min(cost * 128.0 + lane.astype(F32)).astype(jnp.int32) & 127

    mine_second = (gz & 1) == 1

    def of_mine(values):
        return jnp.where(mine_second, values[1], values[0])

    code_a = _chain(lax.shift_right_logical(best, 5) & 3, groups[0][3])
    code_b = _chain(lax.shift_right_logical(best, 3) & 3, groups[1][3])
    order = jnp.where(mine_second, _chain(best & 7, [jnp.int32(o) for o in ORDERS + ORDERS[:2]]), ORDERS[0])
    code = of_mine((code_a, code_b))

    def round_of(edge):
        return lax.shift_right_logical(order, 2 * _colour(code, edge)) & 3

    hot = of_mine([g[0] for g in groups])
    spots = [of_mine([g[2][i] for g in groups]) for i in range(3)]
    mine, pred, p1 = [of_mine([g[i] for g in groups]) for i in (4, 5, 6)]
    c8, c32 = (gz & 1) * 8, (gz & 1) * 32
    base = of_mine(bases)

    def inner(g, s):
        return lax.shift_right_logical(corners[2, base + g * stride + s], 5) & 3

    star = [round_of(7 + i) for i in range(3)]
    is_hot = me == hot
    at = jnp.maximum(mine, 0)
    out_round = round_of(at)
    in_round = round_of(_pick(at == 0, 6, at - 1))
    my_succ = succ[c8 + me]
    swaps_here = jnp.logical_not(is_hot) & (swap[c8 + me] == 1)
    swap_at = _pick(swaps_here, _pick(at == 0, star[0], _pick(at == p1, star[1], star[2])), -1)
    places, arrives, slots = [], [], []
    for k in range(ROUNDS):
        hot_partner = sum(_pick(star[i] == k, spots[i], 0) for i in range(3))
        kind = _pick(swap_at == k, 3, _pick(out_round == k, 1, _pick(in_round == k, 2, 0)))
        partner = _pick(swap_at == k, hot, _pick(out_round == k, my_succ, pred))
        kind = _pick(is_hot, 3, kind)
        partner = _pick(is_hot, hot_partner, partner)
        way = me ^ partner
        up = ((kind == 1) & (me < partner)) | ((kind == 2) & (partner < me))
        plan[k] = _pick(kind == 0, 0, _pick(kind == 3, way, _pick(up, 7 + way, 14 + way)))
        slot = jnp.int32(0)
        place = jnp.int32(0)
        for s in range(PER_DEV):
            slot = slot + _pick(own[c32 + me * PER_DEV + s] == partner, s, 0)
            place = place + _pick(own[c32 + partner * PER_DEV + s] == me, inner(partner, s), 0)
        slots.append(jnp.minimum(slot, PER_DEV - 1))
        places.append(place)
        arrives.append((kind == 2) | (kind == 3))
    pays = (pay0, pay1, pay2)
    u_copies = [pltpu.make_async_copy(f0.at[slots[k]], ubox.at[k], sems.at[k, 3]) for k in range(ROUNDS)]
    copies = [
        pltpu.make_async_copy(field.at[slots[k]], pays[k].at[pl.ds(f * BOX, BOX)], sems.at[k, f])
        for k in range(ROUNDS)
        for f, field in enumerate((f1, f2, f3))
    ]
    for copy in u_copies + copies:
        copy.start()
    for q in range(PER_DEV):
        source = jnp.int32(0)
        for s in range(PER_DEV):
            source = source + _pick((own[c32 + me * PER_DEV + s] == me) & (inner(me, s) == q), s, 0)
        for k in range(ROUNDS):
            source = source + _pick(arrives[k] & (places[k] == q), 4 + k, 0)
        plan[4 + q] = source
    plan[3] = jnp.int32(0)
    for k in range(ROUNDS):
        u_copies[k].wait()
        halve(ubox.at[k], rows8.at[k], pays[k].at[pl.ds(3 * BOX, HALF)])
    for copy in copies:
        copy.wait()


def halve(box, tmp, out):
    lane = iota(1)
    is_odd = ((lax.shift_right_logical(lane, 5) + lane) & 1) == 1
    for j in range(8):
        tmp[j] = box[:, j * 128 : j * 128 + 128]
    for h in range(2):
        for j in range(8):
            lower = tmp[j, pl.ds(16 * h, 8, stride=2), :]
            upper = tmp[j, pl.ds(16 * h + 1, 8, stride=2), :]
            out[8 * h : 8 * h + 8, j * 128 : j * 128 + 128] = jnp.where(is_odd, lower, upper)


def plan_and_pack(corners, fields):
    hbm = pl.BlockSpec(memory_space=pltpu.HBM)
    smem = pl.BlockSpec(memory_space=pltpu.SMEM)
    vmem = pl.BlockSpec(memory_space=pltpu.VMEM)
    pay = jax.ShapeDtypeStruct((3 * BOX + HALF, BOX * BOX), F32)
    return pl.pallas_call(
        plan_kernel,
        out_shape=(jax.ShapeDtypeStruct((8,), jnp.int32), pay, pay, pay),
        in_specs=[hbm] * 5,
        out_specs=(smem, vmem, vmem, vmem),
        scratch_shapes=[
            pltpu.SMEM(corners.shape, jnp.int32),
            pltpu.SMEM((64,), jnp.int32),
            pltpu.SMEM((16,), jnp.int32),
            pltpu.SMEM((16,), jnp.int32),
            pltpu.SMEM((16,), jnp.int32),
            pltpu.VMEM((ROUNDS, BOX, BOX * BOX), F32),
            pltpu.VMEM((ROUNDS, 8, BOX, 128), F32),
            pltpu.SemaphoreType.DMA((ROUNDS, 4)),
            pltpu.SemaphoreType.DMA,
        ],
        compiler_params=pltpu.CompilerParams(vmem_limit_bytes=60 * MIB),
        name="plan",
    )(corners, *fields)


def swap_round(branch, pay):
    def stay(x):
        return x

    def move(pairs, x):
        return lax.ppermute(x, "gy", pairs)

    branches = [stay]
    for r in range(1, 8):
        branches.append(functools.partial(move, [(i, i ^ r) for i in range(8)]))
    for r in range(1, 8):
        branches.append(functools.partial(move, [(i, i ^ r) for i in range(8) if i < i ^ r]))
    for r in range(1, 8):
        branches.append(functools.partial(move, [(i, i ^ r) for i in range(8) if i > i ^ r]))
    return lax.switch(branch, branches, pay)


def iota(dim):
    return lax.broadcasted_iota(jnp.int32, (8, 128), dim)


def lroll(v, shift):
    shift %= 128
    return pltpu.roll(v, shift, 1) if shift else v


def sroll(v, shift):
    shift %= 8
    return pltpu.roll(v, shift, 0) if shift else v


U1, B1, B0, F0, A0, F1, A1 = range(7)
WIDTH = (5, 5, 4, 4, 4, 3, 3)
LAYERS = [(n, i) for n in range(7) for i in range(3 if n < 2 else 2)]


def odd_cell():
    return ((iota(0) + iota(1)) & 1) == 1


def assemble_kernel(plan, f0, f1, f2, f3, r0, r1, r2, home, even, odd, ubox, uhalf, rows8, raw, tmp, sems):
    fields = (f1, f2, f3)
    gots = (r0, r1, r2)
    rows = pl.ds(3 * BOX, HALF)
    for q in range(PER_DEV):
        source = plan[4 + q]

        @pl.when(source < 4)
        def _():
            box = jnp.minimum(source, 3)
            pltpu.make_async_copy(f0.at[box], ubox.at[q], sems.at[3, q]).start()
            for f in range(3):
                pltpu.make_async_copy(fields[f].at[box], raw.at[f, q], sems.at[f, q]).start()

        for k in range(ROUNDS):

            @pl.when(source == 4 + k)
            def _():
                pltpu.make_async_copy(gots[k].at[rows], uhalf.at[q], sems.at[3, q]).start()
                for f in range(3):
                    pltpu.make_async_copy(gots[k].at[pl.ds(f * BOX, BOX)], raw.at[f, q], sems.at[f, q]).start()

    lane = iota(1)
    m64 = (lane & 64) != 0
    m32 = (lane & 32) != 0
    is_odd = odd_cell()

    def relayout(load):
        for t in range(4):
            for jj in range(2):
                j = 2 * t + jj
                a = [load(k, slice(j * 128, (j + 1) * 128)) for k in range(4)]
                n0 = jnp.where(m64, lroll(a[2], 64), a[0])
                n2 = jnp.where(m64, a[2], lroll(a[0], 64))
                n1 = jnp.where(m64, lroll(a[3], 64), a[1])
                n3 = jnp.where(m64, a[3], lroll(a[1], 64))
                b = [
                    jnp.where(m32, lroll(n1, 32), n0),
                    jnp.where(m32, n1, lroll(n0, 96)),
                    jnp.where(m32, lroll(n3, 32), n2),
                    jnp.where(m32, n3, lroll(n2, 96)),
                ]
                for q in range(4):
                    y = jj * 4 + q
                    tmp[t, y * 8 : y * 8 + 8, :] = b[q]

    for f in range(3):
        for q in range(PER_DEV):
            pltpu.make_async_copy(f0.at[0], raw.at[f, q], sems.at[f, q]).wait()

        def step(i, carry):
            xt = pl.multiple_of(i * 8, 8)
            relayout(lambda k, lanes: raw[f, k, pl.ds(xt, 8), lanes])
            for t in range(4):
                ys = slice(t * 8, t * 8 + 8)
                for x in range(0, 8, 2):
                    lower = tmp[t, pl.ds(x, 8, stride=8), :]
                    upper = tmp[t, pl.ds(x + 1, 8, stride=8), :]
                    j = i * 4 + x // 2
                    home[(F1, A1, B1)[f], j, ys, :] = jnp.where(is_odd, lower, upper)
                    home[(F0, A0, B0)[f], j, ys, :] = jnp.where(is_odd, upper, lower)
            return carry

        lax.fori_loop(0, 4, step, 0, unroll=2)

    for q in range(PER_DEV):
        mine = plan[4 + q] < 4

        @pl.when(mine)
        def _():
            pltpu.make_async_copy(f0.at[0], ubox.at[q], sems.at[3, q]).wait()
            halve(ubox.at[q], rows8.at[q], uhalf.at[q])

        @pl.when(jnp.logical_not(mine))
        def _():
            pltpu.make_async_copy(r0.at[rows], uhalf.at[q], sems.at[3, q]).wait()

    for i in range(2):
        relayout(lambda k, lanes: uhalf[k, 8 * i : 8 * i + 8, lanes])
        for t in range(4):
            for x in range(8):
                home[U1, i * 8 + x, t * 8 : t * 8 + 8, :] = tmp[t, pl.ds(x, 8, stride=8), :]

    low = (lax.axis_index("gx") & 1) == 1
    for k, (n, i) in enumerate(LAYERS):
        last = HALF - (3 if n < 2 else 2) + i
        even[k] = home[n, jnp.where(low, i, last)]
        odd[k] = home[n, jnp.where(low, last, i)]


def assemble(plan, fields, gots):
    any_spec = pl.BlockSpec(memory_space=pl.ANY)
    hbm = pl.BlockSpec(memory_space=pltpu.HBM)
    vmem = pl.BlockSpec(memory_space=pltpu.VMEM)
    face = jax.ShapeDtypeStruct((16, BOX, 128), F32)
    return pl.pallas_call(
        assemble_kernel,
        out_shape=(jax.ShapeDtypeStruct((7, HALF, BOX, 128), F32), face, face),
        in_specs=[pl.BlockSpec(memory_space=pltpu.SMEM)] + [hbm] * 4 + [any_spec] * 3,
        out_specs=(vmem, vmem, vmem),
        scratch_shapes=[
            pltpu.VMEM((PER_DEV, BOX, BOX * BOX), F32),
            pltpu.VMEM((PER_DEV, HALF, BOX * BOX), F32),
            pltpu.VMEM((PER_DEV, 8, BOX, 128), F32),
            pltpu.VMEM((3, PER_DEV, BOX, BOX * BOX), F32),
            pltpu.VMEM((4, 64, 128), F32),
            pltpu.SemaphoreType.DMA((4, PER_DEV)),
        ],
        compiler_params=pltpu.CompilerParams(vmem_limit_bytes=12 * MIB),
        name="assemble",
    )(plan, *fields, *gots)


def halo_of(axis, count, even, odd):
    i = lax.axis_index(axis)
    low_first = (i & 1) == 1
    low = jnp.where(i > 0, jnp.where(low_first, even, odd), 0.0)
    high = jnp.where(i < count - 1, jnp.where(low_first, odd, even), 0.0)
    return low, high


def x_halo_tiles(even, odd, t):
    ys = slice(t * 8, t * 8 + 8)
    pairs = {}
    for k, (n, i) in enumerate(LAYERS):
        low, high = halo_of("gx", N_GX, even[k, ys, :], odd[k, ys, :])
        pairs.setdefault(SIDE - (3 if n < 2 else 2) + i, {})[n] = low
        pairs.setdefault(SIDE + HALF + i, {})[n] = high
    return pairs


def pack_y_kernel(home, x_even, x_odd, even, odd):
    low = (lax.axis_index("gy") & 1) == 1
    sub = iota(0)

    def put(at, lo, hi):
        even[at] = jnp.where(low, lo, hi)
        odd[at] = jnp.where(low, hi, lo)

    def put_pairs(k, first, second):
        for i, (near, far) in enumerate((first, second)):
            at = 3 * (k - 1 + i)
            put(at, jnp.where(sub < 5, near[U1], sroll(near[F1], 5)), jnp.where(sub < 5, sroll(far[U1], -3), far[F1]))
            put(at + 1, jnp.where(sub < 5, near[B1], sroll(near[A1], 5)), jnp.where(sub < 5, sroll(far[B1], -3), far[A1]))
            put(at + 2, jnp.where(sub < 4, near[B0], sroll(near[F0], 4)), jnp.where(sub < 4, sroll(far[B0], 4), far[F0]))
        (n0, f0), (n1, f1) = first, second
        lo = jnp.where(sub < 4, n0[A0], sroll(n1[A0], 4))
        hi = jnp.where(sub < 4, sroll(f0[A0], 4), f1[A0])
        put(3 * SENT + k // 2, lo, hi)

    halo = (x_halo_tiles(x_even, x_odd, 0), x_halo_tiles(x_even, x_odd, 3))
    zero = jnp.zeros((8, 128), F32)

    def tiles(k):
        inside = SIDE <= k < SIDE + HALF
        out = []
        for near_far in range(2):
            ys = slice(24 * near_far, 24 * near_far + 8)
            if inside:
                out.append([home[n, k - SIDE, ys, :] for n in range(7)])
            else:
                out.append([halo[near_far][k].get(n, zero) for n in range(7)])
        return out

    for k in range(1, PAIRS - 1, 2):
        put_pairs(k, tiles(k), tiles(k + 1))


PAD = (8, 8, 8, 0, 0, 0, 0)


def pack_z_kernel(home, x_even, x_odd, y_even, y_odd, u1, b1, b0, f0, a0, f1, a1, face):
    outs = (u1, b1, b0, f0, a0, f1, a1)

    def copy(j, carry):
        for n in range(7):
            outs[n][j + SIDE, PAD[n] + 8 : PAD[n] + 40, :] = home[n, j]
        return carry

    lax.fori_loop(0, HALF, copy, 0, unroll=2)
    for t in range(4):
        for k, tiles in x_halo_tiles(x_even, x_odd, t).items():
            for n, tile in tiles.items():
                outs[n][k, PAD[n] + 8 + t * 8 : PAD[n] + 16 + t * 8, :] = tile

    def halo(m, carry):
        l3, h3 = halo_of("gy", N_GY, y_even[3 * SENT + m], y_odd[3 * SENT + m])
        for i in range(2):
            k = 2 * m + 1 + i
            (l0, h0), (l1, h1), (l2, h2) = [
                halo_of("gy", N_GY, y_even[3 * k - 3 + w], y_odd[3 * k - 3 + w]) for w in range(3)
            ]
            lows = (sroll(l0, 3), sroll(l1, 3), sroll(l2, 4), l2, sroll(l3, 4) if i == 0 else l3, l0, l1)
            highs = (h0, h1, h2, sroll(h2, 4), h3 if i == 0 else sroll(h3, 4), sroll(h0, 3), sroll(h1, 3))
            for n in range(7):
                outs[n][k, PAD[n] : PAD[n] + 8, :] = lows[n]
                outs[n][k, PAD[n] + 40 : PAD[n] + 48, :] = highs[n]
        return carry

    lax.fori_loop(0, SENT // 2, halo, 0)
    lane = iota(1)
    place = lane & 63

    def pack(k, carry):
        for v in range(3):
            both = []
            for w in range(2):
                t = 2 * v + w
                at = 64 * w
                group = None
                ends = []
                for n in range(7):
                    tile = outs[n][k, PAD[n] + t * 8 : PAD[n] + t * 8 + 8, :]
                    ends.append((lroll(tile, at + WIDTH[n]), at + 2 * WIDTH[n]))
                    at += 2 * WIDTH[n]
                group = ends[-1][0]
                for tile, end in reversed(ends[:-1]):
                    group = jnp.where(place < end - 64 * w, tile, group)
                both.append(group)
            face[k - 1, v] = jnp.where(lane < 64, both[0], both[1])
        return carry

    lax.fori_loop(1, PAIRS - 1, pack, 0, unroll=2)


def sweep_kernel(u1, b1, b0, f0, a0, f1, a1, z_even, z_odd, sol, res, um0, um1, ua0, ua1, ba0, ba1, fax, co, dg):
    lane = iota(1)
    first, last = lane == 0, lane == 127
    place = lane & 63
    is_odd = odd_cell()
    u = ((um0, ua0), (um1, ua1))
    b = ((b0, ba0), (b1, ba1))
    fa = (((f0, a0), (fax.at[0], fax.at[1])), ((f1, a1), (fax.at[2], fax.at[3])))
    starts = [2 * sum(WIDTH[:n]) for n in range(7)]
    high_part = functools.reduce(
        jnp.logical_or, [(place >= starts[n]) & (place < starts[n] + WIDTH[n]) for n in range(7)]
    )
    aux = (ua1, ba1, ba0, fax.at[0], fax.at[1], fax.at[2], fax.at[3])

    def unpack(k, carry):
        for v in range(3):
            low, high = halo_of("gz", N_GZ, z_even[k - 1, v], z_odd[k - 1, v])
            both = jnp.where(high_part, low, high)
            for w in range(2):
                t = 2 * v + w
                for n in range(7):
                    aux[n][k, PAD[n] + t * 8 : PAD[n] + t * 8 + 8, :] = lroll(both, -(64 * w + starts[n] + WIDTH[n]))
        return carry

    um1[...] = u1[...]
    lax.fori_loop(1, PAIRS - 1, unpack, 0, unroll=2)

    def around(c, field, k, t, spans):
        r = 8 + t * 8
        main, side = field[1 - c]
        m, a = main[k, r : r + 8, :], side[k, r : r + 8, :]
        m1, a1 = lroll(m, 1), lroll(a, 1)
        m2, a2 = lroll(m, 127), lroll(a, 127)
        below = (jnp.where(first, a1, m1), jnp.where(first, m1, a1))
        above = (jnp.where(last, a2, m2), jnp.where(last, m2, a2))
        out = []
        for s in spans:
            ref = (main, side)[s]
            back, ahead = ref[k - 1, r : r + 8, :], ref[k + 1, r : r + 8, :]
            beside = jnp.where(is_odd, back, ahead) if c else jnp.where(is_odd, ahead, back)
            out.append(((m, a)[s], beside, ref[k, r - 1 : r + 7, :], ref[k, r + 1 : r + 9, :], below[s], above[s]))
        return out

    def coefs(k, carry):
        for c in range(2):
            for t in range(6):
                rows = slice(t * 8, 8 + t * 8)
                near = around(c, b, k, t, (0, 1))
                for s in range(2):
                    mid = b[c][s][k, 8 + t * 8 : 16 + t * 8, :]
                    f, a = [ref[k, rows, :] for ref in fa[c][s]]
                    faces = [0.5 * (mid + v) for v in near[s]]
                    diag = a + (faces[0] + faces[1]) + (faces[2] + faces[3]) + (faces[4] + faces[5])
                    inverse = jnp.where(mid > 0, 1.0 / diag, 0.0)
                    for n in range(6):
                        co[c, s, n, k - 1, rows, :] = faces[n] * inverse
                    co[c, s, 6, k - 1, rows, :] = f * inverse
                    if s == 0:
                        dg[c, k - 1, rows, :] = diag
        return carry

    lax.fori_loop(1, PAIRS - 1, coefs, 0)

    def update(c, k, t, spans):
        rows = slice(t * 8, 8 + t * 8)
        new = []
        for s, v in zip(spans, around(c, u, k, t, spans)):
            w = [co[c, s, n, k - 1, rows, :] for n in range(7)]
            x = w[0] * v[0] + w[1] * v[1]
            y = w[2] * v[2] + w[3] * v[3]
            z = w[4] * v[4] + w[5] * v[5]
            new.append(w[6] + ((x + y) + z))
        return new

    for half in range(2 * SWEEPS):
        c = half % 2

        def sweep(k, carry):
            for t in range(6):
                for s, new in enumerate(update(c, k, t, (0, 1))):
                    u[c][s][k, 8 + t * 8 : 16 + t * 8, :] = new
            return carry

        out = half // 2
        lax.fori_loop(1 + out, PAIRS - 1 - out, sweep, 0, unroll=2)

    def finish(j, carry):
        k = j + SIDE
        for t in range(1, 5):
            ys = slice(t * 8 - 8, t * 8)
            rows = slice(t * 8, t * 8 + 8)
            now = [u[c][0][k, 8 + t * 8 : 16 + t * 8, :] for c in range(2)]
            rest = [dg[c, k - 1, rows, :] * (update(c, k, t, (0,))[0] - now[c]) for c in range(2)]
            for ref, (v0, v1) in ((sol, now), (res, rest)):
                ref[2 * j, ys, :] = jnp.where(is_odd, v1, v0)
                ref[2 * j + 1, ys, :] = jnp.where(is_odd, v0, v1)
        return carry

    lax.fori_loop(0, HALF, finish, 0, unroll=2)


def on_vmem(kernel, out_shape, scratch, name, limit, *args):
    vmem = pl.BlockSpec(memory_space=pltpu.VMEM)
    return pl.pallas_call(
        kernel,
        out_shape=out_shape,
        in_specs=[vmem] * len(args),
        out_specs=tuple([vmem] * len(out_shape)),
        scratch_shapes=scratch,
        compiler_params=pltpu.CompilerParams(vmem_limit_bytes=limit * MIB),
        name=name,
    )(*args)


def pack_y(home, x_even, x_odd):
    face = jax.ShapeDtypeStruct((3 * SENT + SENT // 2, 8, 128), F32)
    return on_vmem(pack_y_kernel, (face, face), [], "pack_y", 10, home, x_even, x_odd)


def pack_z(home, x_even, x_odd, y_even, y_odd):
    grown = [jax.ShapeDtypeStruct((PAIRS, 48 + 2 * PAD[n], 128), F32) for n in range(7)]
    face = jax.ShapeDtypeStruct((SENT, 3, 8, 128), F32)
    return on_vmem(pack_z_kernel, (*grown, face), [], "pack_z", 16, home, x_even, x_odd, y_even, y_odd)


def sweeps(grown, z_even, z_odd):
    block = jax.ShapeDtypeStruct((BOX, BOX, 128), F32)
    padded = pltpu.VMEM((PAIRS, 64, 128), F32)
    scratch = [padded] * 6 + [
        pltpu.VMEM((4, PAIRS, 48, 128), F32),
        pltpu.VMEM((2, 2, 7, PAIRS - 2, 48, 128), F32),
        pltpu.VMEM((2, PAIRS - 2, 48, 128), F32),
    ]
    return on_vmem(sweep_kernel, (block, block), scratch, "sweeps", 40, *grown, z_even, z_odd)


def exchange(axis, count, even, odd):
    pairs = []
    for start in (0, 1):
        step = []
        for i in range(start, count, 2):
            j = (i + 1) % count
            step += [(i, j), (j, i)]
        pairs.append(step)
    return lax.ppermute(even, axis, pairs[0]), lax.ppermute(odd, axis, pairs[1])


def per_device(solution_old, right_side, acoef, bcoef, corners):
    fields = (solution_old, right_side, acoef, bcoef)
    plan, *pays = plan_and_pack(corners, fields)
    gots = [swap_round(plan[k], pays[k]) for k in range(ROUNDS)]
    home, even, odd = assemble(plan, fields, gots)
    x_even, x_odd = exchange("gx", N_GX, even, odd)
    y_even, y_odd = exchange("gy", N_GY, *pack_y(home, x_even, x_odd))
    *grown, face = pack_z(home, x_even, x_odd, y_even, y_odd)
    z_even, z_odd = exchange("gz", N_GZ, face, face)
    return sweeps(grown, z_even, z_odd)


def solution(mesh):
    boxes = P(("gx", "gy", "gz"), None, None)
    block = P("gx", "gy", "gz")
    return jax.shard_map(
        per_device,
        mesh=mesh,
        in_specs=(boxes, boxes, boxes, boxes, P()),
        out_specs=(block, block),
        check_vma=False,
    )
```

profile of v0, /device:TPU:1, one launch (start us, length us, event | category | flops | bytes accessed | tf_op | source)
XLA Modules:
  0.0 111.5 jit_solution(965849885352940611)
XLA Ops:
  0.6 3.8 %plan.1 = (s32[8]{0:T(128)}, f32[112,1024]{1,0:T(8,128)S(1)}, f32[112,1024]{1,0:T(8,128)S(1)}, f32[112,1024]{1,0:T(8,128)S(1)}) custom-call(s32[3,1024]{1,0:T(4,128)} %table.1, f32[4,32,1024]{2,1,0:T(8,128)} %f0.3, f32[4,32,1024]{2,1,0:T(8,128)} %f1.3, f32[4,32,1024]{2,1,0:T(8,128)} %f2.3, f32[4,32,1024]{2,1,0:T(8,128)} %f3.3), custom_call_target="tpu_custom_call" | custom-call | tf_op jit(solution)/shard_map/plan/pallas_call | solution.py:229
  4.5 1.4 %fusion = (s32[1]{0:T(128)}, s32[1]{0:T(128)}, s32[1]{0:T(128)}) fusion(s32[8]{0:T(128)} %get-tuple-element.154.plan), kind=kLoop, calls=%fused_computation | loop fusion | bytes 24 | tf_op jit(solution)/shard_map/slice | solution.py:665
  7.8 40.9 %conditional.4 = (f32[112,1024]{1,0:T(8,128)S(1)}) conditional(s32[]{:T(128)} %bitcast.1, f32[112,1024]{1,0:T(8,128)S(1)} %get-tuple-element.156, f32[112,1024]{1,0:T(8,128)S(1)} %get-tuple-element.156, f32[112,1024]{1,0:T(8,128)S(1)} %get-tuple-element.156, f32[112,1024]{1,0:T(8,128)S(1)} %get-tuple-element.156, ...), branch_computations={%region_22.0_spmd, %region_23.0_spmd, %region_24.0_spmd, %region_2... | conditional | bytes 2752560 | solution.py:264
  8.0 1.3 %collective-permute-start.36 = (f32[112,1024]{1,0:T(8,128)S(1)}, f32[112,1024]{1,0:T(8,128)S(1)}, u32[]{:S(2)}, u32[]{:S(2)}) collective-permute-start(f32[112,1024]{1,0:T(8,128)S(1)} %param.38), channel_id=1, source_target_pairs={{16,0},{24,8},{48,32},{56,40},{17,1},{25,9},{49,33},{57,41},{18,2}... | collective-permute-start | bytes 1376264 | tf_op jit(solution)/shard_map/cond/branch_16_fun/ppermute | solution.py:255
  9.3 39.3 %collective-permute-done.36 = f32[112,1024]{1,0:T(8,128)S(1)} collective-permute-done((f32[112,1024]{1,0:T(8,128)S(1)}, f32[112,1024]{1,0:T(8,128)S(1)}, u32[]{:S(2)}, u32[]{:S(2)}) %collective-permute-start.36) | collective-permute-done | bytes 458784 | tf_op jit(solution)/shard_map/cond/branch_16_fun/ppermute | solution.py:255
  48.6 0.0 copy-start
  48.6 0.0 copy-start.2
  48.7 0.0 copy-start.3
  48.7 11.7 %conditional.3 = (f32[112,1024]{1,0:T(8,128)S(1)}) conditional(s32[]{:T(128)} %bitcast, f32[112,1024]{1,0:T(8,128)S(1)} %get-tuple-element.155, f32[112,1024]{1,0:T(8,128)S(1)} %get-tuple-element.155, f32[112,1024]{1,0:T(8,128)S(1)} %get-tuple-element.155, f32[112,1024]{1,0:T(8,128)S(1)} %get-tuple-element.155, ...), branch_computations={%region_0.0_spmd, %region_1.0_spmd, %region_2.0_spmd, %region_3.0_... | conditional | bytes 2752560 | solution.py:264
  48.7 1.4 %collective-permute-start.13 = (f32[112,1024]{1,0:T(8,128)S(1)}, f32[112,1024]{1,0:T(8,128)S(1)}, u32[]{:S(2)}, u32[]{:S(2)}) collective-permute-start(f32[112,1024]{1,0:T(8,128)S(1)} %param.14), channel_id=1, source_target_pairs={{0,56},{8,48},{16,40},{24,32},{1,57},{9,49},{17,41},{25,33},{2,58}... | collective-permute-start | bytes 1376264 | tf_op jit(solution)/shard_map/cond/branch_14_fun/ppermute | solution.py:255
  50.2 10.1 %collective-permute-done.13 = f32[112,1024]{1,0:T(8,128)S(1)} collective-permute-done((f32[112,1024]{1,0:T(8,128)S(1)}, f32[112,1024]{1,0:T(8,128)S(1)}, u32[]{:S(2)}, u32[]{:S(2)}) %collective-permute-start.13) | collective-permute-done | bytes 458784 | tf_op jit(solution)/shard_map/cond/branch_14_fun/ppermute | solution.py:255
  60.4 5.5 %assemble.1 = (f32[7,16,32,128]{3,2,1,0:T(8,128)S(1)}, f32[16,32,128]{2,1,0:T(8,128)S(1)}, f32[16,32,128]{2,1,0:T(8,128)S(1)}) custom-call(s32[8]{0:T(128)S(1)} %copy-done.4, f32[4,32,1024]{2,1,0:T(8,128)S(1)} %copy-done, f32[4,32,1024]{2,1,0:T(8,128)S(1)} %copy-done.1, f32[4,32,1024]{2,1,0:T(8,128)S(1)} %copy-done.2, f32[4,32,1024]{2,1,0:T(8,128)S(1)} %copy-done.3, ...), custom_call_target="tpu_custom_call" | custom-call | tf_op jit(solution)/shard_map/assemble/pallas_call | solution.py:385
  65.9 0.1 collective-permute-start.63
  66.0 0.1 collective-permute-start.64
  66.1 7.5 %collective-permute-done.63.x_even = f32[16,32,128]{2,1,0:T(8,128)S(1)} collective-permute-done((f32[16,32,128]{2,1,0:T(8,128)S(1)}, f32[16,32,128]{2,1,0:T(8,128)S(1)}, u32[]{:S(2)}, u32[]{:S(2)}) %collective-permute-start.63) | collective-permute-done | bytes 262176 | tf_op jit(solution)/shard_map/ppermute | solution.py:659
  73.6 0.1 pack_y.1
  73.7 0.1 collective-permute-start.65
  73.8 3.6 %collective-permute-start.66 = (f32[70,8,128]{2,1,0:T(8,128)S(1)}, f32[70,8,128]{2,1,0:T(8,128)S(1)}, u32[]{:S(2)}, u32[]{:S(2)}) collective-permute-start(f32[70,8,128]{2,1,0:T(8,128)S(1)} %get-tuple-element.162), channel_id=1, source_target_pairs={{8,16},{16,8},{24,32},{32,24},{40,48},{48,40},{56,0},{0,56},{9,17}... | collective-permute-start | bytes 860168 | tf_op jit(solution)/shard_map/ppermute | solution.py:659
  77.4 2.3 %collective-permute-done.65.y_even = f32[70,8,128]{2,1,0:T(8,128)S(1)} collective-permute-done((f32[70,8,128]{2,1,0:T(8,128)S(1)}, f32[70,8,128]{2,1,0:T(8,128)S(1)}, u32[]{:S(2)}, u32[]{:S(2)}) %collective-permute-start.65) | collective-permute-done | bytes 286752 | tf_op jit(solution)/shard_map/ppermute | solution.py:659
  79.7 4.3 %collective-permute-done.66.y_odd = f32[70,8,128]{2,1,0:T(8,128)S(1)} collective-permute-done((f32[70,8,128]{2,1,0:T(8,128)S(1)}, f32[70,8,128]{2,1,0:T(8,128)S(1)}, u32[]{:S(2)}, u32[]{:S(2)}) %collective-permute-start.66) | collective-permute-done | bytes 286752 | tf_op jit(solution)/shard_map/ppermute | solution.py:659
  84.0 2.0 %pack_z.1 = (f32[22,64,128]{2,1,0:T(8,128)S(1)}, f32[22,64,128]{2,1,0:T(8,128)S(1)}, f32[22,64,128]{2,1,0:T(8,128)S(1)}, f32[22,48,128]{2,1,0:T(8,128)S(1)}, f32...) custom-call(f32[7,16,32,128]{3,2,1,0:T(8,128)S(1)} %get-tuple-elemen, ...), custom_call_target="tpu_custom_call" | custom-call | tf_op jit(solution)/shard_map/pack_z/pallas_call | solution.py:618
  86.0 9.0 %collective-permute-start.68 = (f32[20,3,8,128]{3,2,1,0:T(8,128)S(1)}, f32[20,3,8,128]{3,2,1,0:T(8,128)S(1)}, u32[]{:S(2)}, u32[]{:S(2)}) collective-permute-start(f32[20,3,8,128]{3,2,1,0:T(8,128)S(1)} %get-tuple-element.170), channel_id=1, source_target_pairs={{1,2},{2,1},{3,4},{4,3},{5,6},{6,5},{7,0},{0,7},{9,10},{10,9},{11,... | collective-permute-start | bytes 737288 | tf_op jit(solution)/shard_map/ppermute | solution.py:659
  95.1 3.9 %collective-permute-done.68.z_odd = f32[20,3,8,128]{3,2,1,0:T(8,128)S(1)} collective-permute-done((f32[20,3,8,128]{3,2,1,0:T(8,128)S(1)}, f32[20,3,8,128]{3,2,1,0:T(8,128)S(1)}, u32[]{:S(2)}, u32[]{:S(2)}) %collective-permute-start.68) | collective-permute-done | bytes 245792 | tf_op jit(solution)/shard_map/ppermute | solution.py:659
  98.9 12.5 %sweeps.1 = (f32[32,32,128]{2,1,0:T(8,128)}, f32[32,32,128]{2,1,0:T(8,128)}) custom-call(f32[22,64,128]{2,1,0:T(8,128)S(1)} %get-tuple-element.163.u1, f32[22,64,128]{2,1,0:T(8,128)S(1)} %get-tuple-element.164.b1, f32[22,64,128]{2,1,0:T(8,128)S(1)} %get-tuple-element.165.b0, f32[22,48,128]{2,1,0:T(8,128)S(1)} %get-tuple-element.166.f0, ...), custom_call_target="tpu_custom_call" | custom-call | tf_op jit(solution)/shard_map/sweeps/pallas_call | solution.py:618
  (13 shorter events, 0.1 us)
Async XLA Ops:
  8.0 40.6 %collective-permute-start.36 = (f32[112,1024]{1,0:T(8,128)S(1)}, f32[112,1024]{1,0:T(8,128)S(1)}, u32[]{:S(2)}, u32[]{:S(2)}) collective-permute-start(f32[112,1024]{1,0:T(8,128)S(1)} %param.38), channel_id=1, source_target_pairs={{16,0},{24,8},{48,32},{56,40},{17,1},{25,9},{49,33},{57,41},{18,2}... | collective-permute-start | bytes 1376264 | tf_op jit(solution)/shard_map/cond/branch_16_fun/ppermute | solution.py:255
  48.6 11.7 %copy-start = (f32[4,32,1024]{2,1,0:T(8,128)S(1)}, f32[4,32,1024]{2,1,0:T(8,128)}, u32[]{:S(2)}) copy-start(f32[4,32,1024]{2,1,0:T(8,128)} %f0.3) | copy-start | bytes 1572868
  48.6 11.7 %copy-start.1 = (f32[4,32,1024]{2,1,0:T(8,128)S(1)}, f32[4,32,1024]{2,1,0:T(8,128)}, u32[]{:S(2)}) copy-start(f32[4,32,1024]{2,1,0:T(8,128)} %f1.3) | copy-start | bytes 1572868
  48.6 11.7 %copy-start.2 = (f32[4,32,1024]{2,1,0:T(8,128)S(1)}, f32[4,32,1024]{2,1,0:T(8,128)}, u32[]{:S(2)}) copy-start(f32[4,32,1024]{2,1,0:T(8,128)} %f2.3) | copy-start | bytes 1572868
  48.7 11.7 %copy-start.3 = (f32[4,32,1024]{2,1,0:T(8,128)S(1)}, f32[4,32,1024]{2,1,0:T(8,128)}, u32[]{:S(2)}) copy-start(f32[4,32,1024]{2,1,0:T(8,128)} %f3.3) | copy-start | bytes 1572868
  48.7 11.7 %copy-start.4 = (s32[8]{0:T(128)S(1)}, s32[8]{0:T(128)}, u32[]{:S(2)}) copy-start(s32[8]{0:T(128)} %get-tuple-element.154.plan) | copy-start | bytes 100
  48.7 11.5 %collective-permute-start.13 = (f32[112,1024]{1,0:T(8,128)S(1)}, f32[112,1024]{1,0:T(8,128)S(1)}, u32[]{:S(2)}, u32[]{:S(2)}) collective-permute-start(f32[112,1024]{1,0:T(8,128)S(1)} %param.14), channel_id=1, source_target_pairs={{0,56},{8,48},{16,40},{24,32},{1,57},{9,49},{17,41},{25,33},{2,58}... | collective-permute-start | bytes 1376264 | tf_op jit(solution)/shard_map/cond/branch_14_fun/ppermute | solution.py:255
  65.9 7.7 %collective-permute-start.63 = (f32[16,32,128]{2,1,0:T(8,128)S(1)}, f32[16,32,128]{2,1,0:T(8,128)S(1)}, u32[]{:S(2)}, u32[]{:S(2)}) collective-permute-start(f32[16,32,128]{2,1,0:T(8,128)S(1)} %get-tuple-element.159), channel_id=1, source_target_pairs={{0,64},{64,0},{128,192},{192,128},{1,65},{65,1},{129,193},{193,129... | collective-permute-start | bytes 786440 | tf_op jit(solution)/shard_map/ppermute | solution.py:659
  66.0 7.6 %collective-permute-start.64 = (f32[16,32,128]{2,1,0:T(8,128)S(1)}, f32[16,32,128]{2,1,0:T(8,128)S(1)}, u32[]{:S(2)}, u32[]{:S(2)}) collective-permute-start(f32[16,32,128]{2,1,0:T(8,128)S(1)} %get-tuple-element.160), channel_id=1, source_target_pairs={{64,128},{128,64},{192,0},{0,192},{65,129},{129,65},{193,1},{1,193... | collective-permute-start | bytes 786440 | tf_op jit(solution)/shard_map/ppermute | solution.py:659
  73.7 6.0 %collective-permute-start.65 = (f32[70,8,128]{2,1,0:T(8,128)S(1)}, f32[70,8,128]{2,1,0:T(8,128)S(1)}, u32[]{:S(2)}, u32[]{:S(2)}) collective-permute-start(f32[70,8,128]{2,1,0:T(8,128)S(1)} %get-tuple-element.161), channel_id=1, source_target_pairs={{0,8},{8,0},{16,24},{24,16},{32,40},{40,32},{48,56},{56,48},{1,9},... | collective-permute-start | bytes 860168 | tf_op jit(solution)/shard_map/ppermute | solution.py:659
  73.8 10.2 %collective-permute-start.66 = (f32[70,8,128]{2,1,0:T(8,128)S(1)}, f32[70,8,128]{2,1,0:T(8,128)S(1)}, u32[]{:S(2)}, u32[]{:S(2)}) collective-permute-start(f32[70,8,128]{2,1,0:T(8,128)S(1)} %get-tuple-element.162), channel_id=1, source_target_pairs={{8,16},{16,8},{24,32},{32,24},{40,48},{48,40},{56,0},{0,56},{9,17}... | collective-permute-start | bytes 860168 | tf_op jit(solution)/shard_map/ppermute | solution.py:659
  86.0 12.9 %collective-permute-start.68 = (f32[20,3,8,128]{3,2,1,0:T(8,128)S(1)}, f32[20,3,8,128]{3,2,1,0:T(8,128)S(1)}, u32[]{:S(2)}, u32[]{:S(2)}) collective-permute-start(f32[20,3,8,128]{3,2,1,0:T(8,128)S(1)} %get-tuple-element.170), channel_id=1, source_target_pairs={{1,2},{2,1},{3,4},{4,3},{5,6},{6,5},{7,0},{0,7},{9,10},{10,9},{11,... | collective-permute-start | bytes 737288 | tf_op jit(solution)/shard_map/ppermute | solution.py:659
  95.1 3.9 %collective-permute-start.67 = (f32[20,3,8,128]{3,2,1,0:T(8,128)S(1)}, f32[20,3,8,128]{3,2,1,0:T(8,128)S(1)}, u32[]{:S(2)}, u32[]{:S(2)}) collective-permute-start(f32[20,3,8,128]{3,2,1,0:T(8,128)S(1)} %get-tuple-element.170), channel_id=1, source_target_pairs={{0,1},{1,0},{2,3},{3,2},{4,5},{5,4},{6,7},{7,6},{8,9},{9,8},{10,11... | collective-permute-start | bytes 737288 | tf_op jit(solution)/shard_map/ppermute | solution.py:659
where the time goes:
time: 113 us; the launch traced here: 111 us
  waiting for transfers between devices  67.4 us (60%)
  Pallas kernels  23.9 us (21%)
  starting transfers between devices  15.7 us (14%)
  between operations  2.66 us (2%)
  local copies, waits for them, and re-layouts  1.47 us (1%)
    ppermute x2, waiting for transfers between devices, move(): return lax.ppermute(x, 'gy', pairs)  49.4 us
    pallas_call x3, Pallas kernels, on_vmem(): pl.pallas_call(kernel, out_shape=out_shape, in_specs=[vmem] * len(args),...  14.6 us
    ppermute x3, starting transfers between devices, exchange(): lax.ppermute(odd, axis, pairs[1])  12.7 us
    ppermute x3, waiting for transfers between devices, exchange(): lax.ppermute(even, axis, pairs[0])  9.85 us
    ppermute x3, waiting for transfers between devices, exchange(): lax.ppermute(odd, axis, pairs[1])  8.18 us
    pallas_call x1, Pallas kernels, assemble(): pl.pallas_call(assemble_kernel, out_shape=(jax.ShapeDtypeStruct((7, HALF,...  5.48 us
    pallas_call x1, Pallas kernels, plan_and_pack(): pl.pallas_call(plan_kernel, out_shape=(jax.ShapeDtypeStruct((8,), jnp.int...  3.82 us
    ppermute x2, starting transfers between devices, move(): return lax.ppermute(x, 'gy', pairs)  2.74 us
  transfers between devices with their start and end apart: 8, of which 6 were waited for; matrix products, arithmetic and copies ran while one was open for 0% of the time, Pallas kernels for 0%

commit v1 on v0

--- a/solution.py
+++ b/solution.py
@@ -15,7 +15,6 @@
 HALF = BOX // 2
 SIDE = 3
 PAIRS = HALF + 2 * SIDE
-SENT = PAIRS - 2
 SWEEPS = 2
 F32 = jnp.float32
 MIB = 1024 * 1024
@@ -287,7 +286,39 @@
     return ((iota(0) + iota(1)) & 1) == 1
 
 
-def assemble_kernel(plan, f0, f1, f2, f3, r0, r1, r2, home, even, odd, ubox, uhalf, rows8, raw, tmp, sems):
+def face_rows(first, second):
+    sub = iota(0)
+    out = []
+    for near, far in (first, second):
+        out.append((jnp.where(sub < 5, near[U1], sroll(near[F1], 5)), jnp.where(sub < 5, sroll(far[U1], -3), far[F1])))
+        out.append((jnp.where(sub < 5, near[B1], sroll(near[A1], 5)), jnp.where(sub < 5, sroll(far[B1], -3), far[A1])))
+        out.append((jnp.where(sub < 4, near[B0], sroll(near[F0], 4)), jnp.where(sub < 4, sroll(far[B0], 4), far[F0])))
+    (n0, f0), (n1, f1) = first, second
+    lo = jnp.where(sub < 4, n0[A0], sroll(n1[A0], 4))
+    hi = jnp.where(sub < 4, sroll(f0[A0], 4), f1[A0])
+    return out + [(lo, hi)]
+
+
+def face_lanes(first, second):
+    lane = iota(1)
+    place = lane & 63
+    both = []
+    for w, tiles in enumerate((first, second)):
+        at = 0
+        ends = []
+        for n in range(7):
+            ends.append((lroll(tiles[n], 64 * w + at + WIDTH[n]), at + 2 * WIDTH[n]))
+            at += 2 * WIDTH[n]
+        group = ends[-1][0]
+        for tile, end in reversed(ends[:-1]):
+            group = jnp.where(place < end, tile, group)
+        both.append(group)
+    return jnp.where(lane < 64, both[0], both[1])
+
+
+def assemble_kernel(
+    plan, f0, f1, f2, f3, r0, r1, r2, home, even, odd, y_even, y_odd, z_face, ubox, uhalf, rows8, raw, tmp, sems
+):
     fields = (f1, f2, f3)
     gots = (r0, r1, r2)
     rows = pl.ds(3 * BOX, HALF)
@@ -376,17 +407,39 @@
         even[k] = home[n, jnp.where(low, i, last)]
         odd[k] = home[n, jnp.where(low, last, i)]
 
+    low_y = (lax.axis_index("gy") & 1) == 1
+
+    def faces(m, carry):
+        tiles = [[[home[n, 2 * m + i, 8 * t : 8 * t + 8, :] for n in range(7)] for t in range(4)] for i in range(2)]
+        for w, (lo, hi) in enumerate(face_rows(*[(tiles[i][0], tiles[i][3]) for i in range(2)])):
+            y_even[7 * m + w] = jnp.where(low_y, lo, hi)
+            y_odd[7 * m + w] = jnp.where(low_y, hi, lo)
+        for i in range(2):
+            for v in range(2):
+                z_face[2 * m + i, v] = face_lanes(tiles[i][2 * v], tiles[i][2 * v + 1])
+        return carry
+
+    lax.fori_loop(0, HALF // 2, faces, 0)
+
 
 def assemble(plan, fields, gots):
     any_spec = pl.BlockSpec(memory_space=pl.ANY)
     hbm = pl.BlockSpec(memory_space=pltpu.HBM)
     vmem = pl.BlockSpec(memory_space=pltpu.VMEM)
     face = jax.ShapeDtypeStruct((16, BOX, 128), F32)
+    rows = jax.ShapeDtypeStruct((7 * HALF // 2, 8, 128), F32)
     return pl.pallas_call(
         assemble_kernel,
-        out_shape=(jax.ShapeDtypeStruct((7, HALF, BOX, 128), F32), face, face),
+        out_shape=(
+            jax.ShapeDtypeStruct((7, HALF, BOX, 128), F32),
+            face,
+            face,
+            rows,
+            rows,
+            jax.ShapeDtypeStruct((HALF, 2, 8, 128), F32),
+        ),
         in_specs=[pl.BlockSpec(memory_space=pltpu.SMEM)] + [hbm] * 4 + [any_spec] * 3,
-        out_specs=(vmem, vmem, vmem),
+        out_specs=(vmem,) * 6,
         scratch_shapes=[
             pltpu.VMEM((PER_DEV, BOX, BOX * BOX), F32),
             pltpu.VMEM((PER_DEV, HALF, BOX * BOX), F32),
@@ -418,101 +471,63 @@
     return pairs
 
 
-def pack_y_kernel(home, x_even, x_odd, even, odd):
+EDGES = (1, 2, SIDE + HALF, SIDE + HALF + 1)
+
+
+def edge_y_kernel(x_even, x_odd, even, odd):
     low = (lax.axis_index("gy") & 1) == 1
-    sub = iota(0)
-
-    def put(at, lo, hi):
-        even[at] = jnp.where(low, lo, hi)
-        odd[at] = jnp.where(low, hi, lo)
-
-    def put_pairs(k, first, second):
-        for i, (near, far) in enumerate((first, second)):
-            at = 3 * (k - 1 + i)
-            put(at, jnp.where(sub < 5, near[U1], sroll(near[F1], 5)), jnp.where(sub < 5, sroll(far[U1], -3), far[F1]))
-            put(at + 1, jnp.where(sub < 5, near[B1], sroll(near[A1], 5)), jnp.where(sub < 5, sroll(far[B1], -3), far[A1]))
-            put(at + 2, jnp.where(sub < 4, near[B0], sroll(near[F0], 4)), jnp.where(sub < 4, sroll(far[B0], 4), far[F0]))
-        (n0, f0), (n1, f1) = first, second
-        lo = jnp.where(sub < 4, n0[A0], sroll(n1[A0], 4))
-        hi = jnp.where(sub < 4, sroll(f0[A0], 4), f1[A0])
-        put(3 * SENT + k // 2, lo, hi)
-
-    halo = (x_halo_tiles(x_even, x_odd, 0), x_halo_tiles(x_even, x_odd, 3))
-    zero = jnp.zeros((8, 128), F32)
-
-    def tiles(k):
-        inside = SIDE <= k < SIDE + HALF
-        out = []
-        for near_far in range(2):
-            ys = slice(24 * near_far, 24 * near_far + 8)
-            if inside:
-                out.append([home[n, k - SIDE, ys, :] for n in range(7)])
-            else:
-                out.append([halo[near_far][k].get(n, zero) for n in range(7)])
-        return out
-
-    for k in range(1, PAIRS - 1, 2):
-        put_pairs(k, tiles(k), tiles(k + 1))
+    near, far = x_halo_tiles(x_even, x_odd, 0), x_halo_tiles(x_even, x_odd, 3)
+    for m in range(2):
+        for w, (lo, hi) in enumerate(face_rows(*[(near[k], far[k]) for k in EDGES[2 * m : 2 * m + 2]])):
+            even[7 * m + w] = jnp.where(low, lo, hi)
+            odd[7 * m + w] = jnp.where(low, hi, lo)
 
 
 PAD = (8, 8, 8, 0, 0, 0, 0)
 
 
-def pack_z_kernel(home, x_even, x_odd, y_even, y_odd, u1, b1, b0, f0, a0, f1, a1, face):
+def edge_z_kernel(home, x_even, x_odd, y_even, y_odd, e_even, e_odd, u1, b1, b0, f0, a0, f1, a1, edge):
     outs = (u1, b1, b0, f0, a0, f1, a1)
 
-    def copy(j, carry):
-        for n in range(7):
-            outs[n][j + SIDE, PAD[n] + 8 : PAD[n] + 40, :] = home[n, j]
-        return carry
-
-    lax.fori_loop(0, HALF, copy, 0, unroll=2)
-    for t in range(4):
-        for k, tiles in x_halo_tiles(x_even, x_odd, t).items():
-            for n, tile in tiles.items():
-                outs[n][k, PAD[n] + 8 + t * 8 : PAD[n] + 16 + t * 8, :] = tile
-
-    def halo(m, carry):
-        l3, h3 = halo_of("gy", N_GY, y_even[3 * SENT + m], y_odd[3 * SENT + m])
-        for i in range(2):
-            k = 2 * m + 1 + i
-            (l0, h0), (l1, h1), (l2, h2) = [
-                halo_of("gy", N_GY, y_even[3 * k - 3 + w], y_odd[3 * k - 3 + w]) for w in range(3)
-            ]
+    def halo(even, odd, m, pairs):
+        low_high = [halo_of("gy", N_GY, even[7 * m + w], odd[7 * m + w]) for w in range(7)]
+        l3, h3 = low_high[6]
+        for i, k in enumerate(pairs):
+            (l0, h0), (l1, h1), (l2, h2) = low_high[3 * i : 3 * i + 3]
             lows = (sroll(l0, 3), sroll(l1, 3), sroll(l2, 4), l2, sroll(l3, 4) if i == 0 else l3, l0, l1)
             highs = (h0, h1, h2, sroll(h2, 4), h3 if i == 0 else sroll(h3, 4), sroll(h0, 3), sroll(h1, 3))
             for n in range(7):
                 outs[n][k, PAD[n] : PAD[n] + 8, :] = lows[n]
                 outs[n][k, PAD[n] + 40 : PAD[n] + 48, :] = highs[n]
+
+    def tiles(k, t):
+        return [outs[n][k, PAD[n] + t * 8 : PAD[n] + t * 8 + 8, :] for n in range(7)]
+
+    def copy(m, carry):
+        for i in range(2):
+            for n in range(7):
+                outs[n][2 * m + i + SIDE, PAD[n] + 8 : PAD[n] + 40, :] = home[n, 2 * m + i]
+        halo(y_even, y_odd, m, (2 * m + SIDE, 2 * m + SIDE + 1))
+        for i in range(2):
+            k = 2 * m + i + SIDE
+            edge[12 + 2 * m + i] = face_lanes(tiles(k, 0), tiles(k, 5))
         return carry
 
-    lax.fori_loop(0, SENT // 2, halo, 0)
-    lane = iota(1)
-    place = lane & 63
-
-    def pack(k, carry):
+    lax.fori_loop(0, HALF // 2, copy, 0)
+    for t in range(4):
+        for k, fields in x_halo_tiles(x_even, x_odd, t).items():
+            for n, tile in fields.items():
+                outs[n][k, PAD[n] + 8 + t * 8 : PAD[n] + 16 + t * 8, :] = tile
+    for m in range(2):
+        halo(e_even, e_odd, m, EDGES[2 * m : 2 * m + 2])
+    for i, k in enumerate(EDGES):
         for v in range(3):
-            both = []
-            for w in range(2):
-                t = 2 * v + w
-                at = 64 * w
-                group = None
-                ends = []
-                for n in range(7):
-                    tile = outs[n][k, PAD[n] + t * 8 : PAD[n] + t * 8 + 8, :]
-                    ends.append((lroll(tile, at + WIDTH[n]), at + 2 * WIDTH[n]))
-                    at += 2 * WIDTH[n]
-                group = ends[-1][0]
-                for tile, end in reversed(ends[:-1]):
-                    group = jnp.where(place < end - 64 * w, tile, group)
-                both.append(group)
-            face[k - 1, v] = jnp.where(lane < 64, both[0], both[1])
-        return carry
-
-    lax.fori_loop(1, PAIRS - 1, pack, 0, unroll=2)
-
-
-def sweep_kernel(u1, b1, b0, f0, a0, f1, a1, z_even, z_odd, sol, res, um0, um1, ua0, ua1, ba0, ba1, fax, co, dg):
+            edge[3 * i + v] = face_lanes(tiles(k, 2 * v), tiles(k, 2 * v + 1))
+
+
+def sweep_kernel(
+    u1, b1, b0, f0, a0, f1, a1, z_even, z_odd, e_even, e_odd, sol, res, um0, um1, ua0, ua1, ba0, ba1, fax, co, dg
+):
     lane = iota(1)
     first, last = lane == 0, lane == 127
     place = lane & 63
@@ -526,18 +541,24 @@
     )
     aux = (ua1, ba1, ba0, fax.at[0], fax.at[1], fax.at[2], fax.at[3])
 
-    def unpack(k, carry):
+    def unpack(k, even, odd, spots):
+        low, high = halo_of("gz", N_GZ, even, odd)
+        both = jnp.where(high_part, low, high)
+        for w, t in enumerate(spots):
+            for n in range(7):
+                aux[n][k, PAD[n] + t * 8 : PAD[n] + t * 8 + 8, :] = lroll(both, -(64 * w + starts[n] + WIDTH[n]))
+
+    def unpack_pair(j, carry):
+        for v in range(2):
+            unpack(j + SIDE, z_even[j, v], z_odd[j, v], (1 + 2 * v, 2 + 2 * v))
+        unpack(j + SIDE, e_even[12 + j], e_odd[12 + j], (0, 5))
+        return carry
+
+    um1[...] = u1[...]
+    lax.fori_loop(0, HALF, unpack_pair, 0, unroll=2)
+    for i, k in enumerate(EDGES):
         for v in range(3):
-            low, high = halo_of("gz", N_GZ, z_even[k - 1, v], z_odd[k - 1, v])
-            both = jnp.where(high_part, low, high)
-            for w in range(2):
-                t = 2 * v + w
-                for n in range(7):
-                    aux[n][k, PAD[n] + t * 8 : PAD[n] + t * 8 + 8, :] = lroll(both, -(64 * w + starts[n] + WIDTH[n]))
-        return carry
-
-    um1[...] = u1[...]
-    lax.fori_loop(1, PAIRS - 1, unpack, 0, unroll=2)
+            unpack(k, e_even[3 * i + v], e_odd[3 * i + v], (2 * v, 2 * v + 1))
 
     def around(c, field, k, t, spans):
         r = 8 + t * 8
@@ -626,18 +647,18 @@
     )(*args)
 
 
-def pack_y(home, x_even, x_odd):
-    face = jax.ShapeDtypeStruct((3 * SENT + SENT // 2, 8, 128), F32)
-    return on_vmem(pack_y_kernel, (face, face), [], "pack_y", 10, home, x_even, x_odd)
-
-
-def pack_z(home, x_even, x_odd, y_even, y_odd):
+def edge_y(x_even, x_odd):
+    face = jax.ShapeDtypeStruct((14, 8, 128), F32)
+    return on_vmem(edge_y_kernel, (face, face), [], "edge_y", 10, x_even, x_odd)
+
+
+def edge_z(*args):
     grown = [jax.ShapeDtypeStruct((PAIRS, 48 + 2 * PAD[n], 128), F32) for n in range(7)]
-    face = jax.ShapeDtypeStruct((SENT, 3, 8, 128), F32)
-    return on_vmem(pack_z_kernel, (*grown, face), [], "pack_z", 16, home, x_even, x_odd, y_even, y_odd)
-
-
-def sweeps(grown, z_even, z_odd):
+    face = jax.ShapeDtypeStruct((12 + HALF, 8, 128), F32)
+    return on_vmem(edge_z_kernel, (*grown, face), [], "edge_z", 16, *args)
+
+
+def sweeps(grown, *faces):
     block = jax.ShapeDtypeStruct((BOX, BOX, 128), F32)
     padded = pltpu.VMEM((PAIRS, 64, 128), F32)
     scratch = [padded] * 6 + [
@@ -645,7 +666,7 @@
         pltpu.VMEM((2, 2, 7, PAIRS - 2, 48, 128), F32),
         pltpu.VMEM((2, PAIRS - 2, 48, 128), F32),
     ]
-    return on_vmem(sweep_kernel, (block, block), scratch, "sweeps", 40, *grown, z_even, z_odd)
+    return on_vmem(sweep_kernel, (block, block), scratch, "sweeps", 40, *grown, *faces)
 
 
 def exchange(axis, count, even, odd):
@@ -663,12 +684,13 @@
     fields = (solution_old, right_side, acoef, bcoef)
     plan, *pays = plan_and_pack(corners, fields)
     gots = [swap_round(plan[k], pays[k]) for k in range(ROUNDS)]
-    home, even, odd = assemble(plan, fields, gots)
-    x_even, x_odd = exchange("gx", N_GX, even, odd)
-    y_even, y_odd = exchange("gy", N_GY, *pack_y(home, x_even, x_odd))
-    *grown, face = pack_z(home, x_even, x_odd, y_even, y_odd)
-    z_even, z_odd = exchange("gz", N_GZ, face, face)
-    return sweeps(grown, z_even, z_odd)
+    home, even, odd, near_even, near_odd, face = assemble(plan, fields, gots)
+    x = exchange("gx", N_GX, even, odd)
+    y = exchange("gy", N_GY, near_even, near_odd)
+    z = exchange("gz", N_GZ, face, face)
+    y_edges = exchange("gy", N_GY, *edge_y(*x))
+    *grown, edge = edge_z(home, *x, *y, *y_edges)
+    return sweeps(grown, *z, *exchange("gz", N_GZ, edge, edge))
 
 
 def solution(mesh):

time: 113 us -> 107 us (0.947); the launches traced: 111 us -> 109 us
  waiting for transfers between devices: 67.4 us -> 36.2 us
  starting transfers between devices: 15.7 us -> 43.8 us
    ppermute x3 -> x5, starting transfers between devices: 0.19 us -> 23.5 us  [exchange(): lax.ppermute(even, axis, pairs[0])]
    ppermute x2, waiting for transfers between devices: 49.4 us -> 31.4 us  [move(): return lax.ppermute(x, 'gy', pairs)]
    ppermute x3 -> x5, waiting for transfers between devices: 9.85 us -> 0.96 us  [exchange(): lax.ppermute(even, axis, pairs[0])]
    ppermute x2, starting transfers between devices: 2.74 us -> 11.1 us  [move(): return lax.ppermute(x, 'gy', pairs)]
    ppermute x3 -> x5, waiting for transfers between devices: 8.18 us -> 3.82 us  [exchange(): lax.ppermute(odd, axis, pairs[1])]
    ppermute x3 -> x5, starting transfers between devices: 12.7 us -> 9.3 us  [exchange(): lax.ppermute(odd, axis, pairs[1])]
  transfers between devices with their start and end apart: 8 -> 12, of which waited for: 6 -> 5; matrix products, arithmetic and copies ran while one was open for 0% -> 0% of each run, Pallas kernels for 0% -> 1%
where the time goes in v1:
time: 107 us; the launch traced here: 109 us
  starting transfers between devices  43.8 us (41%)
  waiting for transfers between devices  36.2 us (34%)
  Pallas kernels  24 us (22%)
  between operations  2.66 us (2%)
  local copies, waits for them, and re-layouts  1.51 us (1%)
    ppermute x2, waiting for transfers between devices, move(): return lax.ppermute(x, 'gy', pairs)  31.4 us
    ppermute x5, starting transfers between devices, exchange(): lax.ppermute(even, axis, pairs[0])  23.5 us
    pallas_call x3, Pallas kernels, on_vmem(): pl.pallas_call(kernel, out_shape=out_shape, in_specs=[vmem] * len(args),...  13.7 us
    ppermute x2, starting transfers between devices, move(): return lax.ppermute(x, 'gy', pairs)  11.1 us
    ppermute x5, starting transfers between devices, exchange(): lax.ppermute(odd, axis, pairs[1])  9.3 us
    pallas_call x1, Pallas kernels, assemble(): pl.pallas_call(assemble_kernel, out_shape=(jax.ShapeDtypeStruct((7, HALF,...  6.51 us
    ppermute x5, waiting for transfers between devices, exchange(): lax.ppermute(odd, axis, pairs[1])  3.82 us
    pallas_call x1, Pallas kernels, plan_and_pack(): pl.pallas_call(plan_kernel, out_shape=(jax.ShapeDtypeStruct((8,), jnp.int...  3.82 us
  transfers between devices with their start and end apart: 12, of which 5 were waited for; matrix products, arithmetic and copies ran while one was open for 0% of the time, Pallas kernels for 1%

profile of v1, /device:TPU:1, one launch (start us, length us, event | category | flops | bytes accessed | tf_op | source)
XLA Modules:
  0.0 108.6 jit_solution(6633664874218964571)
XLA Ops:
  0.6 3.8 %plan.1 = (s32[8]{0:T(128)}, f32[112,1024]{1,0:T(8,128)S(1)}, f32[112,1024]{1,0:T(8,128)S(1)}, f32[112,1024]{1,0:T(8,128)S(1)}) custom-call(s32[3,1024]{1,0:T(4,128)} %table.1, f32[4,32,1024]{2,1,0:T(8,128)} %f0.3, f32[4,32,1024]{2,1,0:T(8,128)} %f1.3, f32[4,32,1024]{2,1,0:T(8,128)} %f2.3, f32[4,32,1024]{2,1,0:T(8,128)} %f3.3), custom_call_target="tpu_custom_call" | custom-call | tf_op jit(solution)/shard_map/plan/pallas_call | solution.py:228
  4.5 1.4 %fusion = (s32[1]{0:T(128)}, s32[1]{0:T(128)}, s32[1]{0:T(128)}) fusion(s32[8]{0:T(128)} %get-tuple-element.157.plan), kind=kLoop, calls=%fused_computation | loop fusion | bytes 24 | tf_op jit(solution)/shard_map/slice | solution.py:686
  7.7 18.6 %conditional.5 = (f32[112,1024]{1,0:T(8,128)S(1)}) conditional(s32[]{:T(128)} %bitcast.2, f32[112,1024]{1,0:T(8,128)S(1)} %get-tuple-element.160, f32[112,1024]{1,0:T(8,128)S(1)} %get-tuple-element.160, f32[112,1024]{1,0:T(8,128)S(1)} %get-tuple-element.160, f32[112,1024]{1,0:T(8,128)S(1)} %get-tuple-element.160, ...), branch_computations={%region_44.0_spmd, %region_45.0_spmd, %region_46.0_spmd, %region_4... | conditional | bytes 2752560 | solution.py:263
  7.8 9.7 %collective-permute-start.52 = (f32[112,1024]{1,0:T(8,128)S(1)}, f32[112,1024]{1,0:T(8,128)S(1)}, u32[]{:S(2)}, u32[]{:S(2)}) collective-permute-start(f32[112,1024]{1,0:T(8,128)S(1)} %param.55), channel_id=1, source_target_pairs={{0,32},{8,40},{16,48},{24,56},{1,33},{9,41},{17,49},{25,57},{2,34}... | collective-permute-start | bytes 1376264 | tf_op jit(solution)/shard_map/cond/branch_11_fun/ppermute | solution.py:254
  17.5 8.9 %collective-permute-done.52 = f32[112,1024]{1,0:T(8,128)S(1)} collective-permute-done((f32[112,1024]{1,0:T(8,128)S(1)}, f32[112,1024]{1,0:T(8,128)S(1)}, u32[]{:S(2)}, u32[]{:S(2)}) %collective-permute-start.52) | collective-permute-done | bytes 458784 | tf_op jit(solution)/shard_map/cond/branch_11_fun/ppermute | solution.py:254
  26.4 0.2 conditional.4
  26.6 0.0 copy-start
  26.6 0.0 copy-start.1
  26.7 24.1 %conditional.3 = (f32[112,1024]{1,0:T(8,128)S(1)}) conditional(s32[]{:T(128)} %bitcast, f32[112,1024]{1,0:T(8,128)S(1)} %get-tuple-element.158, f32[112,1024]{1,0:T(8,128)S(1)} %get-tuple-element.158, f32[112,1024]{1,0:T(8,128)S(1)} %get-tuple-element.158, f32[112,1024]{1,0:T(8,128)S(1)} %get-tuple-element.158, ...), branch_computations={%region_0.0_spmd, %region_1.0_spmd, %region_2.0_spmd, %region_3.0_... | conditional | bytes 2752560 | solution.py:263
  26.7 1.4 %collective-permute-start.16 = (f32[112,1024]{1,0:T(8,128)S(1)}, f32[112,1024]{1,0:T(8,128)S(1)}, u32[]{:S(2)}, u32[]{:S(2)}) collective-permute-start(f32[112,1024]{1,0:T(8,128)S(1)} %param.17), channel_id=1, source_target_pairs={{16,8},{24,0},{48,40},{56,32},{17,9},{25,1},{49,41},{57,33},{18,10... | collective-permute-start | bytes 1376264 | tf_op jit(solution)/shard_map/cond/branch_17_fun/ppermute | solution.py:254
  28.2 22.5 %collective-permute-done.16 = f32[112,1024]{1,0:T(8,128)S(1)} collective-permute-done((f32[112,1024]{1,0:T(8,128)S(1)}, f32[112,1024]{1,0:T(8,128)S(1)}, u32[]{:S(2)}, u32[]{:S(2)}) %collective-permute-start.16) | collective-permute-done | bytes 458784 | tf_op jit(solution)/shard_map/cond/branch_17_fun/ppermute | solution.py:254
  50.8 6.5 %assemble.1 = (f32[7,16,32,128]{3,2,1,0:T(8,128)S(1)}, f32[16,32,128]{2,1,0:T(8,128)S(1)}, f32[16,32,128]{2,1,0:T(8,128)S(1)}, f32[56,8,128]{2,1,0:T(8,128)S(1)}...) custom-call(s32[8]{0:T(128)S(1)} %copy-done.4, f32[4,32,1024]{2,1,0:T(8,128)S(1)} %copy-done, ...), custom_call_target="tpu_custom_call" | custom-call | tf_op jit(solution)/shard_map/assemble/pallas_call | solution.py:431
  57.3 6.5 %collective-permute-start.63 = (f32[16,32,128]{2,1,0:T(8,128)S(1)}, f32[16,32,128]{2,1,0:T(8,128)S(1)}, u32[]{:S(2)}, u32[]{:S(2)}) collective-permute-start(f32[16,32,128]{2,1,0:T(8,128)S(1)} %get-tuple-element.162), channel_id=1, source_target_pairs={{0,64},{64,0},{128,192},{192,128},{1,65},{65,1},{129,193},{193,129... | collective-permute-start | bytes 786440 | tf_op jit(solution)/shard_map/ppermute | solution.py:680
  63.9 4.5 %collective-permute-start.65 = (f32[56,8,128]{2,1,0:T(8,128)S(1)}, f32[56,8,128]{2,1,0:T(8,128)S(1)}, u32[]{:S(2)}, u32[]{:S(2)}) collective-permute-start(f32[56,8,128]{2,1,0:T(8,128)S(1)} %get-tuple-element.164), channel_id=1, source_target_pairs={{0,8},{8,0},{16,24},{24,16},{32,40},{40,32},{48,56},{56,48},{1,9},... | collective-permute-start | bytes 688136 | tf_op jit(solution)/shard_map/ppermute | solution.py:680
  68.4 5.0 %collective-permute-start.66 = (f32[56,8,128]{2,1,0:T(8,128)S(1)}, f32[56,8,128]{2,1,0:T(8,128)S(1)}, u32[]{:S(2)}, u32[]{:S(2)}) collective-permute-start(f32[56,8,128]{2,1,0:T(8,128)S(1)} %get-tuple-element.165), channel_id=1, source_target_pairs={{8,16},{16,8},{24,32},{32,24},{40,48},{48,40},{56,0},{0,56},{9,17}... | collective-permute-start | bytes 688136 | tf_op jit(solution)/shard_map/ppermute | solution.py:680
  73.4 1.5 %collective-permute-start.67 = (f32[14,8,128]{2,1,0:T(8,128)S(1)}, f32[14,8,128]{2,1,0:T(8,128)S(1)}, u32[]{:S(2)}, u32[]{:S(2)}) collective-permute-start(f32[14,8,128]{2,1,0:T(8,128)S(1)} %get-tuple-element.166), channel_id=1, source_target_pairs={{0,8},{8,0},{16,24},{24,16},{32,40},{40,32},{48,56},{56,48},{1,9},... | collective-permute-start | bytes 172040 | tf_op jit(solution)/shard_map/ppermute | solution.py:680
  74.9 4.3 %collective-permute-start.68 = (f32[14,8,128]{2,1,0:T(8,128)S(1)}, f32[14,8,128]{2,1,0:T(8,128)S(1)}, u32[]{:S(2)}, u32[]{:S(2)}) collective-permute-start(f32[14,8,128]{2,1,0:T(8,128)S(1)} %get-tuple-element.167), channel_id=1, source_target_pairs={{8,16},{16,8},{24,32},{32,24},{40,48},{48,40},{56,0},{0,56},{9,17}... | collective-permute-start | bytes 172040 | tf_op jit(solution)/shard_map/ppermute | solution.py:680
  79.2 2.2 %collective-permute-start.69 = (f32[16,2,8,128]{3,2,1,0:T(8,128)S(1)}, f32[16,2,8,128]{3,2,1,0:T(8,128)S(1)}, u32[]{:S(2)}, u32[]{:S(2)}) collective-permute-start(f32[16,2,8,128]{3,2,1,0:T(8,128)S(1)} %get-tuple-element.175), channel_id=1, source_target_pairs={{0,1},{1,0},{2,3},{3,2},{4,5},{5,4},{6,7},{7,6},{8,9},{9,8},{10,11... | collective-permute-start | bytes 393224 | tf_op jit(solution)/shard_map/ppermute | solution.py:680
  81.5 0.3 collective-permute-done.68.e_odd
  81.8 1.2 %edge_z.1 = (f32[22,64,128]{2,1,0:T(8,128)S(1)}, f32[22,64,128]{2,1,0:T(8,128)S(1)}, f32[22,64,128]{2,1,0:T(8,128)S(1)}, f32[22,48,128]{2,1,0:T(8,128)S(1)}, f32...) custom-call(f32[7,16,32,128]{3,2,1,0:T(8,128)S(1)} %get-tuple-elemen, ...), custom_call_target="tpu_custom_call" | custom-call | tf_op jit(solution)/shard_map/edge_z/pallas_call | solution.py:639
  83.0 8.7 %collective-permute-start.71 = (f32[28,8,128]{2,1,0:T(8,128)S(1)}, f32[28,8,128]{2,1,0:T(8,128)S(1)}, u32[]{:S(2)}, u32[]{:S(2)}) collective-permute-start(f32[28,8,128]{2,1,0:T(8,128)S(1)} %get-tuple-element.176), channel_id=1, source_target_pairs={{0,1},{1,0},{2,3},{3,2},{4,5},{5,4},{6,7},{7,6},{8,9},{9,8},{10,11... | collective-permute-start | bytes 344072 | tf_op jit(solution)/shard_map/ppermute | solution.py:680
  91.6 1.0 collective-permute-done.71.e_even
  92.6 3.5 %collective-permute-done.72.e_odd = f32[28,8,128]{2,1,0:T(8,128)S(1)} collective-permute-done((f32[28,8,128]{2,1,0:T(8,128)S(1)}, f32[28,8,128]{2,1,0:T(8,128)S(1)}, u32[]{:S(2)}, u32[]{:S(2)}) %collective-permute-start.72) | collective-permute-done | bytes 114720 | tf_op jit(solution)/shard_map/ppermute | solution.py:680
  96.1 12.4 %sweeps.1 = (f32[32,32,128]{2,1,0:T(8,128)}, f32[32,32,128]{2,1,0:T(8,128)}) custom-call(f32[22,64,128]{2,1,0:T(8,128)S(1)} %get-tuple-element.168.u1, f32[22,64,128]{2,1,0:T(8,128)S(1)} %get-tuple-element.169.b1, f32[22,64,128]{2,1,0:T(8,128)S(1)} %get-tuple-element.170.b0, f32[22,48,128]{2,1,0:T(8,128)S(1)} %get-tuple-element.171.f0, ...), custom_call_target="tpu_custom_call" | custom-call | tf_op jit(solution)/shard_map/sweeps/pallas_call | solution.py:639
  (21 shorter events, 0.2 us)
Async XLA Ops:
  7.8 18.5 %collective-permute-start.52 = (f32[112,1024]{1,0:T(8,128)S(1)}, f32[112,1024]{1,0:T(8,128)S(1)}, u32[]{:S(2)}, u32[]{:S(2)}) collective-permute-start(f32[112,1024]{1,0:T(8,128)S(1)} %param.55), channel_id=1, source_target_pairs={{0,32},{8,40},{16,48},{24,56},{1,33},{9,41},{17,49},{25,57},{2,34}... | collective-permute-start | bytes 1376264 | tf_op jit(solution)/shard_map/cond/branch_11_fun/ppermute | solution.py:254
  26.6 24.1 %copy-start = (f32[4,32,1024]{2,1,0:T(8,128)S(1)}, f32[4,32,1024]{2,1,0:T(8,128)}, u32[]{:S(2)}) copy-start(f32[4,32,1024]{2,1,0:T(8,128)} %f0.3) | copy-start | bytes 1572868
  26.6 24.1 %copy-start.1 = (f32[4,32,1024]{2,1,0:T(8,128)S(1)}, f32[4,32,1024]{2,1,0:T(8,128)}, u32[]{:S(2)}) copy-start(f32[4,32,1024]{2,1,0:T(8,128)} %f1.3) | copy-start | bytes 1572868
  26.6 24.1 %copy-start.2 = (f32[4,32,1024]{2,1,0:T(8,128)S(1)}, f32[4,32,1024]{2,1,0:T(8,128)}, u32[]{:S(2)}) copy-start(f32[4,32,1024]{2,1,0:T(8,128)} %f2.3) | copy-start | bytes 1572868
  26.7 24.1 %copy-start.3 = (f32[4,32,1024]{2,1,0:T(8,128)S(1)}, f32[4,32,1024]{2,1,0:T(8,128)}, u32[]{:S(2)}) copy-start(f32[4,32,1024]{2,1,0:T(8,128)} %f3.3) | copy-start | bytes 1572868
  26.7 24.1 %copy-start.4 = (s32[8]{0:T(128)S(1)}, s32[8]{0:T(128)}, u32[]{:S(2)}) copy-start(s32[8]{0:T(128)} %get-tuple-element.157.plan) | copy-start | bytes 100
  26.7 24.0 %collective-permute-start.16 = (f32[112,1024]{1,0:T(8,128)S(1)}, f32[112,1024]{1,0:T(8,128)S(1)}, u32[]{:S(2)}, u32[]{:S(2)}) collective-permute-start(f32[112,1024]{1,0:T(8,128)S(1)} %param.17), channel_id=1, source_target_pairs={{16,8},{24,0},{48,40},{56,32},{17,9},{25,1},{49,41},{57,33},{18,10... | collective-permute-start | bytes 1376264 | tf_op jit(solution)/shard_map/cond/branch_17_fun/ppermute | solution.py:254
  57.3 16.0 %collective-permute-start.63 = (f32[16,32,128]{2,1,0:T(8,128)S(1)}, f32[16,32,128]{2,1,0:T(8,128)S(1)}, u32[]{:S(2)}, u32[]{:S(2)}) collective-permute-start(f32[16,32,128]{2,1,0:T(8,128)S(1)} %get-tuple-element.162), channel_id=1, source_target_pairs={{0,64},{64,0},{128,192},{192,128},{1,65},{65,1},{129,193},{193,129... | collective-permute-start | bytes 786440 | tf_op jit(solution)/shard_map/ppermute | solution.py:680
  63.9 9.4 %collective-permute-start.64 = (f32[16,32,128]{2,1,0:T(8,128)S(1)}, f32[16,32,128]{2,1,0:T(8,128)S(1)}, u32[]{:S(2)}, u32[]{:S(2)}) collective-permute-start(f32[16,32,128]{2,1,0:T(8,128)S(1)} %get-tuple-element.163), channel_id=1, source_target_pairs={{64,128},{128,64},{192,0},{0,192},{65,129},{129,65},{193,1},{1,193... | collective-permute-start | bytes 786440 | tf_op jit(solution)/shard_map/ppermute | solution.py:680
  63.9 17.6 %collective-permute-start.65 = (f32[56,8,128]{2,1,0:T(8,128)S(1)}, f32[56,8,128]{2,1,0:T(8,128)S(1)}, u32[]{:S(2)}, u32[]{:S(2)}) collective-permute-start(f32[56,8,128]{2,1,0:T(8,128)S(1)} %get-tuple-element.164), channel_id=1, source_target_pairs={{0,8},{8,0},{16,24},{24,16},{32,40},{40,32},{48,56},{56,48},{1,9},... | collective-permute-start | bytes 688136 | tf_op jit(solution)/shard_map/ppermute | solution.py:680
  68.4 13.1 %collective-permute-start.66 = (f32[56,8,128]{2,1,0:T(8,128)S(1)}, f32[56,8,128]{2,1,0:T(8,128)S(1)}, u32[]{:S(2)}, u32[]{:S(2)}) collective-permute-start(f32[56,8,128]{2,1,0:T(8,128)S(1)} %get-tuple-element.165), channel_id=1, source_target_pairs={{8,16},{16,8},{24,32},{32,24},{40,48},{48,40},{56,0},{0,56},{9,17}... | collective-permute-start | bytes 688136 | tf_op jit(solution)/shard_map/ppermute | solution.py:680
  73.4 8.1 %collective-permute-start.67 = (f32[14,8,128]{2,1,0:T(8,128)S(1)}, f32[14,8,128]{2,1,0:T(8,128)S(1)}, u32[]{:S(2)}, u32[]{:S(2)}) collective-permute-start(f32[14,8,128]{2,1,0:T(8,128)S(1)} %get-tuple-element.166), channel_id=1, source_target_pairs={{0,8},{8,0},{16,24},{24,16},{32,40},{40,32},{48,56},{56,48},{1,9},... | collective-permute-start | bytes 172040 | tf_op jit(solution)/shard_map/ppermute | solution.py:680
  74.9 6.9 %collective-permute-start.68 = (f32[14,8,128]{2,1,0:T(8,128)S(1)}, f32[14,8,128]{2,1,0:T(8,128)S(1)}, u32[]{:S(2)}, u32[]{:S(2)}) collective-permute-start(f32[14,8,128]{2,1,0:T(8,128)S(1)} %get-tuple-element.167), channel_id=1, source_target_pairs={{8,16},{16,8},{24,32},{32,24},{40,48},{48,40},{56,0},{0,56},{9,17}... | collective-permute-start | bytes 172040 | tf_op jit(solution)/shard_map/ppermute | solution.py:680
  79.2 12.4 %collective-permute-start.69 = (f32[16,2,8,128]{3,2,1,0:T(8,128)S(1)}, f32[16,2,8,128]{3,2,1,0:T(8,128)S(1)}, u32[]{:S(2)}, u32[]{:S(2)}) collective-permute-start(f32[16,2,8,128]{3,2,1,0:T(8,128)S(1)} %get-tuple-element.175), channel_id=1, source_target_pairs={{0,1},{1,0},{2,3},{3,2},{4,5},{5,4},{6,7},{7,6},{8,9},{9,8},{10,11... | collective-permute-start | bytes 393224 | tf_op jit(solution)/shard_map/ppermute | solution.py:680
  81.5 10.2 %collective-permute-start.70 = (f32[16,2,8,128]{3,2,1,0:T(8,128)S(1)}, f32[16,2,8,128]{3,2,1,0:T(8,128)S(1)}, u32[]{:S(2)}, u32[]{:S(2)}) collective-permute-start(f32[16,2,8,128]{3,2,1,0:T(8,128)S(1)} %get-tuple-element.175), channel_id=1, source_target_pairs={{1,2},{2,1},{3,4},{4,3},{5,6},{6,5},{7,0},{0,7},{9,10},{10,9},{11,... | collective-permute-start | bytes 393224 | tf_op jit(solution)/shard_map/ppermute | solution.py:680
  83.0 9.6 %collective-permute-start.71 = (f32[28,8,128]{2,1,0:T(8,128)S(1)}, f32[28,8,128]{2,1,0:T(8,128)S(1)}, u32[]{:S(2)}, u32[]{:S(2)}) collective-permute-start(f32[28,8,128]{2,1,0:T(8,128)S(1)} %get-tuple-element.176), channel_id=1, source_target_pairs={{0,1},{1,0},{2,3},{3,2},{4,5},{5,4},{6,7},{7,6},{8,9},{9,8},{10,11... | collective-permute-start | bytes 344072 | tf_op jit(solution)/shard_map/ppermute | solution.py:680
  91.6 4.5 %collective-permute-start.72 = (f32[28,8,128]{2,1,0:T(8,128)S(1)}, f32[28,8,128]{2,1,0:T(8,128)S(1)}, u32[]{:S(2)}, u32[]{:S(2)}) collective-permute-start(f32[28,8,128]{2,1,0:T(8,128)S(1)} %get-tuple-element.176), channel_id=1, source_target_pairs={{1,2},{2,1},{3,4},{4,3},{5,6},{6,5},{7,0},{0,7},{9,10},{10,9},{11,... | collective-permute-start | bytes 344072 | tf_op jit(solution)/shard_map/ppermute | solution.py:680

commit v2 on v1

--- a/solution.py
+++ b/solution.py
@@ -55,7 +55,7 @@
 
 
 def plan_kernel(
-    table, f0, f1, f2, f3, plan, pay0, pay1, pay2, corners, own, succ, swap, spot, ubox, rows8, sems, sem
+    table, f0, f1, f2, f3, go0, go1, go2, plan, pay0, pay1, pay2, corners, own, succ, swap, spot, ubox, rows8, sems, sem
 ):
     whole = pltpu.make_async_copy(table, corners, sem)
     whole.start()
@@ -175,7 +175,7 @@
         partner = _pick(is_hot, hot_partner, partner)
         way = me ^ partner
         up = ((kind == 1) & (me < partner)) | ((kind == 2) & (partner < me))
-        plan[k] = _pick(kind == 0, 0, _pick(kind == 3, way, _pick(up, 7 + way, 14 + way)))
+        (go0, go1, go2)[k][0] = _pick(kind == 0, 0, _pick(kind == 3, way, _pick(up, 7 + way, 14 + way)))
         slot = jnp.int32(0)
         place = jnp.int32(0)
         for s in range(PER_DEV):
@@ -199,8 +199,7 @@
             source = source + _pick((own[c32 + me * PER_DEV + s] == me) & (inner(me, s) == q), s, 0)
         for k in range(ROUNDS):
             source = source + _pick(arrives[k] & (places[k] == q), 4 + k, 0)
-        plan[4 + q] = source
-    plan[3] = jnp.int32(0)
+        plan[q] = source
     for k in range(ROUNDS):
         u_copies[k].wait()
         halve(ubox.at[k], rows8.at[k], pays[k].at[pl.ds(3 * BOX, HALF)])
@@ -227,9 +226,9 @@
     pay = jax.ShapeDtypeStruct((3 * BOX + HALF, BOX * BOX), F32)
     return pl.pallas_call(
         plan_kernel,
-        out_shape=(jax.ShapeDtypeStruct((8,), jnp.int32), pay, pay, pay),
+        out_shape=(*[jax.ShapeDtypeStruct((1,), jnp.int32)] * 3, jax.ShapeDtypeStruct((PER_DEV,), jnp.int32), pay, pay, pay),
         in_specs=[hbm] * 5,
-        out_specs=(smem, vmem, vmem, vmem),
+        out_specs=(smem, smem, smem, smem, vmem, vmem, vmem),
         scratch_shapes=[
             pltpu.SMEM(corners.shape, jnp.int32),
             pltpu.SMEM((64,), jnp.int32),
@@ -279,7 +278,9 @@
 
 U1, B1, B0, F0, A0, F1, A1 = range(7)
 WIDTH = (5, 5, 4, 4, 4, 3, 3)
-LAYERS = [(n, i) for n in range(7) for i in range(3 if n < 2 else 2)]
+LAYERS = [(U1, 0), (U1, 1), (U1, 2), (B1, 1), (B1, 2)]
+LAYERS += [(n, i) for n in (B0, F0, A0) for i in range(2)] + [(F1, 0), (F1, 1), (A1, 1)]
+SHARED = {U1: B1, F1: A1}
 
 
 def odd_cell():
@@ -323,7 +324,7 @@
     gots = (r0, r1, r2)
     rows = pl.ds(3 * BOX, HALF)
     for q in range(PER_DEV):
-        source = plan[4 + q]
+        source = plan[q]
 
         @pl.when(source < 4)
         def _():
@@ -350,10 +351,10 @@
             for jj in range(2):
                 j = 2 * t + jj
                 a = [load(k, slice(j * 128, (j + 1) * 128)) for k in range(4)]
-                n0 = jnp.where(m64, lroll(a[2], 64), a[0])
-                n2 = jnp.where(m64, a[2], lroll(a[0], 64))
-                n1 = jnp.where(m64, lroll(a[3], 64), a[1])
-                n3 = jnp.where(m64, a[3], lroll(a[1], 64))
+                n02 = lroll(jnp.where(m64, a[0], a[2]), 64)
+                n13 = lroll(jnp.where(m64, a[1], a[3]), 64)
+                n0, n2 = jnp.where(m64, n02, a[0]), jnp.where(m64, a[2], n02)
+                n1, n3 = jnp.where(m64, n13, a[1]), jnp.where(m64, a[3], n13)
                 b = [
                     jnp.where(m32, lroll(n1, 32), n0),
                     jnp.where(m32, n1, lroll(n0, 96)),
@@ -384,7 +385,7 @@
         lax.fori_loop(0, 4, step, 0, unroll=2)
 
     for q in range(PER_DEV):
-        mine = plan[4 + q] < 4
+        mine = plan[q] < 4
 
         @pl.when(mine)
         def _():
@@ -403,9 +404,16 @@
 
     low = (lax.axis_index("gx") & 1) == 1
     for k, (n, i) in enumerate(LAYERS):
-        last = HALF - (3 if n < 2 else 2) + i
-        even[k] = home[n, jnp.where(low, i, last)]
-        odd[k] = home[n, jnp.where(low, last, i)]
+        count = 3 if n < 2 else 2
+        low_side, high_side = count - 1 - i, HALF - count + i
+        for t in range(4):
+            ys = slice(t * 8, t * 8 + 8)
+            lo, hi = home[n, low_side, ys, :], home[n, high_side, ys, :]
+            if i == 0 and n in SHARED:
+                lo = jnp.where(is_odd, lo, lroll(home[SHARED[n], low_side, ys, :], 1))
+                hi = jnp.where(is_odd, lroll(home[SHARED[n], high_side, ys, :], 1), hi)
+            even[k, ys, :] = jnp.where(low, lo, hi)
+            odd[k, ys, :] = jnp.where(low, hi, lo)
 
     low_y = (lax.axis_index("gy") & 1) == 1
 
@@ -426,7 +434,7 @@
     any_spec = pl.BlockSpec(memory_space=pl.ANY)
     hbm = pl.BlockSpec(memory_space=pltpu.HBM)
     vmem = pl.BlockSpec(memory_space=pltpu.VMEM)
-    face = jax.ShapeDtypeStruct((16, BOX, 128), F32)
+    face = jax.ShapeDtypeStruct((len(LAYERS), BOX, 128), F32)
     rows = jax.ShapeDtypeStruct((7 * HALF // 2, 8, 128), F32)
     return pl.pallas_call(
         assemble_kernel,
@@ -466,8 +474,12 @@
     pairs = {}
     for k, (n, i) in enumerate(LAYERS):
         low, high = halo_of("gx", N_GX, even[k, ys, :], odd[k, ys, :])
-        pairs.setdefault(SIDE - (3 if n < 2 else 2) + i, {})[n] = low
-        pairs.setdefault(SIDE + HALF + i, {})[n] = high
+        count = 3 if n < 2 else 2
+        spots = (SIDE - count + i, SIDE + HALF + count - 1 - i)
+        for spot, tile in zip(spots, (low, high)):
+            pairs.setdefault(spot, {})[n] = tile
+            if i == 0 and n in SHARED:
+                pairs[spot][SHARED[n]] = lroll(tile, -1)
     return pairs
 
 
@@ -594,7 +606,7 @@
                         dg[c, k - 1, rows, :] = diag
         return carry
 
-    lax.fori_loop(1, PAIRS - 1, coefs, 0)
+    lax.fori_loop(1, PAIRS - 1, coefs, 0, unroll=2)
 
     def update(c, k, t, spans):
         rows = slice(t * 8, 8 + t * 8)
@@ -682,8 +694,8 @@
 
 def per_device(solution_old, right_side, acoef, bcoef, corners):
     fields = (solution_old, right_side, acoef, bcoef)
-    plan, *pays = plan_and_pack(corners, fields)
-    gots = [swap_round(plan[k], pays[k]) for k in range(ROUNDS)]
+    go0, go1, go2, plan, *pays = plan_and_pack(corners, fields)
+    gots = [swap_round(go.reshape(()), pay) for go, pay in zip((go0, go1, go2), pays)]
     home, even, odd, near_even, near_odd, face = assemble(plan, fields, gots)
     x = exchange("gx", N_GX, even, odd)
     y = exchange("gy", N_GY, near_even, near_odd)

time: 107 us -> 107 us (level); the launches traced: 109 us -> 107 us
  starting transfers between devices: 43.8 us -> 46.8 us
  waiting for transfers between devices: 36.2 us -> 33.5 us
  local copies, waits for them, and re-layouts: 1.51 us -> 0.09 us
    ppermute x5, starting transfers between devices: 9.3 us -> 20.7 us  [exchange(): lax.ppermute(odd, axis, pairs[1])]
    ppermute x2, starting transfers between devices: 11.1 us -> 2.74 us  [move(): return lax.ppermute(x, 'gy', pairs)]
    ppermute x2, waiting for transfers between devices: 31.4 us -> 25 us  [move(): return lax.ppermute(x, 'gy', pairs)]
    ppermute x5, waiting for transfers between devices: 3.82 us -> 8.49 us  [exchange(): lax.ppermute(odd, axis, pairs[1])]
    slice x1 -> x0, local copies, waits for them, and re-layouts: 1.42 us -> none  [per_device(): gots = [swap_round(plan[k], pays[k]) for k in range(ROUNDS)]]
  transfers between devices with their start and end apart: 12 -> 12, of which waited for: 5 -> 4; matrix products, arithmetic and copies ran while one was open for 0% -> 0% of each run, Pallas kernels for 1% -> 1%
where the time goes in v2:
time: 107 us
  starting transfers between devices  46.8 us (44%)
  waiting for transfers between devices  33.5 us (31%)
  Pallas kernels  23.2 us (22%)
  between operations  2.64 us (2%)
    ppermute x2, waiting for transfers between devices, move(): return lax.ppermute(x, 'gy', pairs)  25 us
    ppermute x5, starting transfers between devices, exchange(): lax.ppermute(even, axis, pairs[0])  23.4 us
    ppermute x5, starting transfers between devices, exchange(): lax.ppermute(odd, axis, pairs[1])  20.7 us
    pallas_call x3, Pallas kernels, on_vmem(): pl.pallas_call(kernel, out_shape=out_shape, in_specs=[vmem] * len(args),...  13.1 us
    ppermute x5, waiting for transfers between devices, exchange(): lax.ppermute(odd, axis, pairs[1])  8.49 us
    pallas_call x1, Pallas kernels, assemble(): pl.pallas_call(assemble_kernel, out_shape=(jax.ShapeDtypeStruct((7, HALF,...  6.24 us
    pallas_call x1, Pallas kernels, plan_and_pack(): pl.pallas_call(plan_kernel, out_shape=(*[jax.ShapeDtypeStruct((1,), jnp.i...  3.85 us
    ppermute x2, starting transfers between devices, move(): return lax.ppermute(x, 'gy', pairs)  2.74 us
  transfers between devices with their start and end apart: 12, of which 4 were waited for; matrix products, arithmetic and copies ran while one was open for 0% of the time, Pallas kernels for 1%

profile of v2, /device:TPU:1, one launch (start us, length us, event | category | flops | bytes accessed | tf_op | source)
XLA Modules:
  0.0 106.6 jit_solution(8342965966359805812)
XLA Ops:
  0.6 3.8 %plan.1 = (s32[1]{0:T(128)}, s32[1]{0:T(128)}, s32[1]{0:T(128)}, s32[4]{0:T(128)}, f32[112,1024]{1,0:T(8,128)S(1)}, /*index=5*/f32[112,1024]{1,0:T(8,128)S(1)}, f32[112,1024]{1,0:T(8,128)S(1)}) custom-call(s32[3,1024]{1,0:T(4,128)} %table.1, f32[4,32,1024]{2,1,0:T(8,128)} %f0.3, f32[4,32,1024]{2,1,0:T(8,128)} %f1.3, f32[4,32,1024]{2,1,0:T(8,128)} %f2.3, ...), custom_call_target="tpu_custom_call" | custom-call | tf_op jit(solution)/shard_map/plan/pallas_call | solution.py:227
  6.3 18.4 %conditional.5 = (f32[112,1024]{1,0:T(8,128)S(1)}) conditional(s32[]{:T(128)} %bitcast.2, f32[112,1024]{1,0:T(8,128)S(1)} %get-tuple-element.166, f32[112,1024]{1,0:T(8,128)S(1)} %get-tuple-element.166, f32[112,1024]{1,0:T(8,128)S(1)} %get-tuple-element.166, f32[112,1024]{1,0:T(8,128)S(1)} %get-tuple-element.166, ...), branch_computations={%region_44.0_spmd, %region_45.0_spmd, %region_46.0_spmd, %region_4... | conditional | bytes 2752560 | solution.py:262
  6.4 1.3 %collective-permute-start.61 = (f32[112,1024]{1,0:T(8,128)S(1)}, f32[112,1024]{1,0:T(8,128)S(1)}, u32[]{:S(2)}, u32[]{:S(2)}) collective-permute-start(f32[112,1024]{1,0:T(8,128)S(1)} %param.64), channel_id=1, source_target_pairs={{32,16},{40,24},{48,0},{56,8},{33,17},{41,25},{49,1},{57,9},{34,18... | collective-permute-start | bytes 1376264 | tf_op jit(solution)/shard_map/cond/branch_20_fun/ppermute | solution.py:253
  7.7 17.0 %collective-permute-done.61 = f32[112,1024]{1,0:T(8,128)S(1)} collective-permute-done((f32[112,1024]{1,0:T(8,128)S(1)}, f32[112,1024]{1,0:T(8,128)S(1)}, u32[]{:S(2)}, u32[]{:S(2)}) %collective-permute-start.61) | collective-permute-done | bytes 458784 | tf_op jit(solution)/shard_map/cond/branch_20_fun/ppermute | solution.py:253
  24.7 0.2 conditional.4
  25.0 0.0 copy-start.1
  25.0 0.0 copy-start.2
  25.0 9.5 %conditional.3 = (f32[112,1024]{1,0:T(8,128)S(1)}) conditional(s32[]{:T(128)} %bitcast, f32[112,1024]{1,0:T(8,128)S(1)} %get-tuple-element.162, f32[112,1024]{1,0:T(8,128)S(1)} %get-tuple-element.162, f32[112,1024]{1,0:T(8,128)S(1)} %get-tuple-element.162, f32[112,1024]{1,0:T(8,128)S(1)} %get-tuple-element.162, ...), branch_computations={%region_0.0_spmd, %region_1.0_spmd, %region_2.0_spmd, %region_3.0_... | conditional | bytes 2752560 | solution.py:262
  25.1 1.4 %collective-permute-start.9 = (f32[112,1024]{1,0:T(8,128)S(1)}, f32[112,1024]{1,0:T(8,128)S(1)}, u32[]{:S(2)}, u32[]{:S(2)}) collective-permute-start(f32[112,1024]{1,0:T(8,128)S(1)} %param.10), channel_id=1, source_target_pairs={{0,24},{8,16},{32,56},{40,48},{1,25},{9,17},{33,57},{41,49},{2,26}... | collective-permute-start | bytes 1376264 | tf_op jit(solution)/shard_map/cond/branch_10_fun/ppermute | solution.py:253
  26.6 8.0 %collective-permute-done.9 = f32[112,1024]{1,0:T(8,128)S(1)} collective-permute-done((f32[112,1024]{1,0:T(8,128)S(1)}, f32[112,1024]{1,0:T(8,128)S(1)}, u32[]{:S(2)}, u32[]{:S(2)}) %collective-permute-start.9) | collective-permute-done | bytes 458784 | tf_op jit(solution)/shard_map/cond/branch_10_fun/ppermute | solution.py:253
  34.6 6.2 %assemble.1 = (f32[7,16,32,128]{3,2,1,0:T(8,128)S(1)}, f32[14,32,128]{2,1,0:T(8,128)S(1)}, f32[14,32,128]{2,1,0:T(8,128)S(1)}, f32[56,8,128]{2,1,0:T(8,128)S(1)}...) custom-call(s32[4]{0:T(128)S(1)} %copy-done.4, f32[4,32,1024]{2,1,0:T(8,128)S(1)} %copy-done, ...), custom_call_target="tpu_custom_call" | custom-call | tf_op jit(solution)/shard_map/assemble/pallas_call | solution.py:439
  40.9 20.5 %collective-permute-start.63 = (f32[14,32,128]{2,1,0:T(8,128)S(1)}, f32[14,32,128]{2,1,0:T(8,128)S(1)}, u32[]{:S(2)}, u32[]{:S(2)}) collective-permute-start(f32[14,32,128]{2,1,0:T(8,128)S(1)} %get-tuple-element.168), channel_id=1, source_target_pairs={{0,64},{64,0},{128,192},{192,128},{1,65},{65,1},{129,193},{193,129... | collective-permute-start | bytes 688136 | tf_op jit(solution)/shard_map/ppermute | solution.py:692
  61.3 6.7 %collective-permute-start.64 = (f32[14,32,128]{2,1,0:T(8,128)S(1)}, f32[14,32,128]{2,1,0:T(8,128)S(1)}, u32[]{:S(2)}, u32[]{:S(2)}) collective-permute-start(f32[14,32,128]{2,1,0:T(8,128)S(1)} %get-tuple-element.169), channel_id=1, source_target_pairs={{64,128},{128,64},{192,0},{0,192},{65,129},{129,65},{193,1},{1,193... | collective-permute-start | bytes 688136 | tf_op jit(solution)/shard_map/ppermute | solution.py:692
  68.1 6.0 %collective-permute-done.64.x_odd = f32[14,32,128]{2,1,0:T(8,128)S(1)} collective-permute-done((f32[14,32,128]{2,1,0:T(8,128)S(1)}, f32[14,32,128]{2,1,0:T(8,128)S(1)}, u32[]{:S(2)}, u32[]{:S(2)}) %collective-permute-start.64) | collective-permute-done | bytes 229408 | tf_op jit(solution)/shard_map/ppermute | solution.py:692
  74.1 0.1 edge_y.1
  74.2 0.3 collective-permute-start.67
  74.4 0.1 collective-permute-start.68
  74.5 2.5 %collective-permute-start.69 = (f32[16,2,8,128]{3,2,1,0:T(8,128)S(1)}, f32[16,2,8,128]{3,2,1,0:T(8,128)S(1)}, u32[]{:S(2)}, u32[]{:S(2)}) collective-permute-start(f32[16,2,8,128]{3,2,1,0:T(8,128)S(1)} %get-tuple-element.181), channel_id=1, source_target_pairs={{0,1},{1,0},{2,3},{3,2},{4,5},{5,4},{6,7},{7,6},{8,9},{9,8},{10,11... | collective-permute-start | bytes 393224 | tf_op jit(solution)/shard_map/ppermute | solution.py:692
  77.1 10.7 %collective-permute-start.70 = (f32[16,2,8,128]{3,2,1,0:T(8,128)S(1)}, f32[16,2,8,128]{3,2,1,0:T(8,128)S(1)}, u32[]{:S(2)}, u32[]{:S(2)}) collective-permute-start(f32[16,2,8,128]{3,2,1,0:T(8,128)S(1)} %get-tuple-element.181), channel_id=1, source_target_pairs={{1,2},{2,1},{3,4},{4,3},{5,6},{6,5},{7,0},{0,7},{9,10},{10,9},{11,... | collective-permute-start | bytes 393224 | tf_op jit(solution)/shard_map/ppermute | solution.py:692
  87.8 1.2 %edge_z.1 = (f32[22,64,128]{2,1,0:T(8,128)S(1)}, f32[22,64,128]{2,1,0:T(8,128)S(1)}, f32[22,64,128]{2,1,0:T(8,128)S(1)}, f32[22,48,128]{2,1,0:T(8,128)S(1)}, f32...) custom-call(f32[7,16,32,128]{3,2,1,0:T(8,128)S(1)} %get-tuple-elemen, ...), custom_call_target="tpu_custom_call" | custom-call | tf_op jit(solution)/shard_map/edge_z/pallas_call | solution.py:651
  89.0 0.1 collective-permute-start.71
  89.1 3.2 %collective-permute-start.72 = (f32[28,8,128]{2,1,0:T(8,128)S(1)}, f32[28,8,128]{2,1,0:T(8,128)S(1)}, u32[]{:S(2)}, u32[]{:S(2)}) collective-permute-start(f32[28,8,128]{2,1,0:T(8,128)S(1)} %get-tuple-element.182), channel_id=1, source_target_pairs={{1,2},{2,1},{3,4},{4,3},{5,6},{6,5},{7,0},{0,7},{9,10},{10,9},{11,... | collective-permute-start | bytes 344072 | tf_op jit(solution)/shard_map/ppermute | solution.py:692
  92.3 2.5 %collective-permute-done.72.e_odd = f32[28,8,128]{2,1,0:T(8,128)S(1)} collective-permute-done((f32[28,8,128]{2,1,0:T(8,128)S(1)}, f32[28,8,128]{2,1,0:T(8,128)S(1)}, u32[]{:S(2)}, u32[]{:S(2)}) %collective-permute-start.72) | collective-permute-done | bytes 114720 | tf_op jit(solution)/shard_map/ppermute | solution.py:692
  94.8 11.8 %sweeps.1 = (f32[32,32,128]{2,1,0:T(8,128)}, f32[32,32,128]{2,1,0:T(8,128)}) custom-call(f32[22,64,128]{2,1,0:T(8,128)S(1)} %get-tuple-element.174.u1, f32[22,64,128]{2,1,0:T(8,128)S(1)} %get-tuple-element.175.b1, f32[22,64,128]{2,1,0:T(8,128)S(1)} %get-tuple-element.176.b0, f32[22,48,128]{2,1,0:T(8,128)S(1)} %get-tuple-element.177.f0, ...), custom_call_target="tpu_custom_call" | custom-call | tf_op jit(solution)/shard_map/sweeps/pallas_call | solution.py:651
  (20 shorter events, 0.1 us)
Async XLA Ops:
  6.4 18.3 %collective-permute-start.61 = (f32[112,1024]{1,0:T(8,128)S(1)}, f32[112,1024]{1,0:T(8,128)S(1)}, u32[]{:S(2)}, u32[]{:S(2)}) collective-permute-start(f32[112,1024]{1,0:T(8,128)S(1)} %param.64), channel_id=1, source_target_pairs={{32,16},{40,24},{48,0},{56,8},{33,17},{41,25},{49,1},{57,9},{34,18... | collective-permute-start | bytes 1376264 | tf_op jit(solution)/shard_map/cond/branch_20_fun/ppermute | solution.py:253
  25.0 9.6 %copy-start = (f32[4,32,1024]{2,1,0:T(8,128)S(1)}, f32[4,32,1024]{2,1,0:T(8,128)}, u32[]{:S(2)}) copy-start(f32[4,32,1024]{2,1,0:T(8,128)} %f0.3) | copy-start | bytes 1572868
  25.0 9.6 %copy-start.1 = (f32[4,32,1024]{2,1,0:T(8,128)S(1)}, f32[4,32,1024]{2,1,0:T(8,128)}, u32[]{:S(2)}) copy-start(f32[4,32,1024]{2,1,0:T(8,128)} %f1.3) | copy-start | bytes 1572868
  25.0 9.6 %copy-start.2 = (f32[4,32,1024]{2,1,0:T(8,128)S(1)}, f32[4,32,1024]{2,1,0:T(8,128)}, u32[]{:S(2)}) copy-start(f32[4,32,1024]{2,1,0:T(8,128)} %f2.3) | copy-start | bytes 1572868
  25.0 9.6 %copy-start.3 = (f32[4,32,1024]{2,1,0:T(8,128)S(1)}, f32[4,32,1024]{2,1,0:T(8,128)}, u32[]{:S(2)}) copy-start(f32[4,32,1024]{2,1,0:T(8,128)} %f3.3) | copy-start | bytes 1572868
  25.0 9.6 %copy-start.4 = (s32[4]{0:T(128)S(1)}, s32[4]{0:T(128)}, u32[]{:S(2)}) copy-start(s32[4]{0:T(128)} %get-tuple-element.160.plan) | copy-start | bytes 52
  25.1 9.4 %collective-permute-start.9 = (f32[112,1024]{1,0:T(8,128)S(1)}, f32[112,1024]{1,0:T(8,128)S(1)}, u32[]{:S(2)}, u32[]{:S(2)}) collective-permute-start(f32[112,1024]{1,0:T(8,128)S(1)} %param.10), channel_id=1, source_target_pairs={{0,24},{8,16},{32,56},{40,48},{1,25},{9,17},{33,57},{41,49},{2,26}... | collective-permute-start | bytes 1376264 | tf_op jit(solution)/shard_map/cond/branch_10_fun/ppermute | solution.py:253
  40.9 27.2 %collective-permute-start.63 = (f32[14,32,128]{2,1,0:T(8,128)S(1)}, f32[14,32,128]{2,1,0:T(8,128)S(1)}, u32[]{:S(2)}, u32[]{:S(2)}) collective-permute-start(f32[14,32,128]{2,1,0:T(8,128)S(1)} %get-tuple-element.168), channel_id=1, source_target_pairs={{0,64},{64,0},{128,192},{192,128},{1,65},{65,1},{129,193},{193,129... | collective-permute-start | bytes 688136 | tf_op jit(solution)/shard_map/ppermute | solution.py:692
  61.3 12.7 %collective-permute-start.64 = (f32[14,32,128]{2,1,0:T(8,128)S(1)}, f32[14,32,128]{2,1,0:T(8,128)S(1)}, u32[]{:S(2)}, u32[]{:S(2)}) collective-permute-start(f32[14,32,128]{2,1,0:T(8,128)S(1)} %get-tuple-element.169), channel_id=1, source_target_pairs={{64,128},{128,64},{192,0},{0,192},{65,129},{129,65},{193,1},{1,193... | collective-permute-start | bytes 688136 | tf_op jit(solution)/shard_map/ppermute | solution.py:692
  68.0 9.1 %collective-permute-start.65 = (f32[56,8,128]{2,1,0:T(8,128)S(1)}, f32[56,8,128]{2,1,0:T(8,128)S(1)}, u32[]{:S(2)}, u32[]{:S(2)}) collective-permute-start(f32[56,8,128]{2,1,0:T(8,128)S(1)} %get-tuple-element.170), channel_id=1, source_target_pairs={{0,8},{8,0},{16,24},{24,16},{32,40},{40,32},{48,56},{56,48},{1,9},... | collective-permute-start | bytes 688136 | tf_op jit(solution)/shard_map/ppermute | solution.py:692
  68.0 19.8 %collective-permute-start.66 = (f32[56,8,128]{2,1,0:T(8,128)S(1)}, f32[56,8,128]{2,1,0:T(8,128)S(1)}, u32[]{:S(2)}, u32[]{:S(2)}) collective-permute-start(f32[56,8,128]{2,1,0:T(8,128)S(1)} %get-tuple-element.171), channel_id=1, source_target_pairs={{8,16},{16,8},{24,32},{32,24},{40,48},{48,40},{56,0},{0,56},{9,17}... | collective-permute-start | bytes 688136 | tf_op jit(solution)/shard_map/ppermute | solution.py:692
  74.2 13.6 %collective-permute-start.67 = (f32[14,8,128]{2,1,0:T(8,128)S(1)}, f32[14,8,128]{2,1,0:T(8,128)S(1)}, u32[]{:S(2)}, u32[]{:S(2)}) collective-permute-start(f32[14,8,128]{2,1,0:T(8,128)S(1)} %get-tuple-element.172), channel_id=1, source_target_pairs={{0,8},{8,0},{16,24},{24,16},{32,40},{40,32},{48,56},{56,48},{1,9},... | collective-permute-start | bytes 172040 | tf_op jit(solution)/shard_map/ppermute | solution.py:692
  74.4 13.4 %collective-permute-start.68 = (f32[14,8,128]{2,1,0:T(8,128)S(1)}, f32[14,8,128]{2,1,0:T(8,128)S(1)}, u32[]{:S(2)}, u32[]{:S(2)}) collective-permute-start(f32[14,8,128]{2,1,0:T(8,128)S(1)} %get-tuple-element.173), channel_id=1, source_target_pairs={{8,16},{16,8},{24,32},{32,24},{40,48},{48,40},{56,0},{0,56},{9,17}... | collective-permute-start | bytes 172040 | tf_op jit(solution)/shard_map/ppermute | solution.py:692
  74.5 17.8 %collective-permute-start.69 = (f32[16,2,8,128]{3,2,1,0:T(8,128)S(1)}, f32[16,2,8,128]{3,2,1,0:T(8,128)S(1)}, u32[]{:S(2)}, u32[]{:S(2)}) collective-permute-start(f32[16,2,8,128]{3,2,1,0:T(8,128)S(1)} %get-tuple-element.181), channel_id=1, source_target_pairs={{0,1},{1,0},{2,3},{3,2},{4,5},{5,4},{6,7},{7,6},{8,9},{9,8},{10,11... | collective-permute-start | bytes 393224 | tf_op jit(solution)/shard_map/ppermute | solution.py:692
  77.1 15.2 %collective-permute-start.70 = (f32[16,2,8,128]{3,2,1,0:T(8,128)S(1)}, f32[16,2,8,128]{3,2,1,0:T(8,128)S(1)}, u32[]{:S(2)}, u32[]{:S(2)}) collective-permute-start(f32[16,2,8,128]{3,2,1,0:T(8,128)S(1)} %get-tuple-element.181), channel_id=1, source_target_pairs={{1,2},{2,1},{3,4},{4,3},{5,6},{6,5},{7,0},{0,7},{9,10},{10,9},{11,... | collective-permute-start | bytes 393224 | tf_op jit(solution)/shard_map/ppermute | solution.py:692
  89.0 3.3 %collective-permute-start.71 = (f32[28,8,128]{2,1,0:T(8,128)S(1)}, f32[28,8,128]{2,1,0:T(8,128)S(1)}, u32[]{:S(2)}, u32[]{:S(2)}) collective-permute-start(f32[28,8,128]{2,1,0:T(8,128)S(1)} %get-tuple-element.182), channel_id=1, source_target_pairs={{0,1},{1,0},{2,3},{3,2},{4,5},{5,4},{6,7},{7,6},{8,9},{9,8},{10,11... | collective-permute-start | bytes 344072 | tf_op jit(solution)/shard_map/ppermute | solution.py:692
  89.1 5.7 %collective-permute-start.72 = (f32[28,8,128]{2,1,0:T(8,128)S(1)}, f32[28,8,128]{2,1,0:T(8,128)S(1)}, u32[]{:S(2)}, u32[]{:S(2)}) collective-permute-start(f32[28,8,128]{2,1,0:T(8,128)S(1)} %get-tuple-element.182), channel_id=1, source_target_pairs={{1,2},{2,1},{3,4},{4,3},{5,6},{6,5},{7,0},{0,7},{9,10},{10,9},{11,... | collective-permute-start | bytes 344072 | tf_op jit(solution)/shard_map/ppermute | solution.py:692

commit v3 on v2

--- a/solution.py
+++ b/solution.py
@@ -55,10 +55,13 @@
 
 
 def plan_kernel(
-    table, f0, f1, f2, f3, go0, go1, go2, plan, pay0, pay1, pay2, corners, own, succ, swap, spot, ubox, rows8, sems, sem
+    table, f0, f1, f2, f3, go0, go1, go2, plan, pay0, pay1, pay2, corners, own, succ, swap, spot, boxes, rows8, sems, sem
 ):
     whole = pltpu.make_async_copy(table, corners, sem)
     whole.start()
+    copies = [pltpu.make_async_copy(field, boxes.at[f], sems.at[f]) for f, field in enumerate((f1, f2, f3, f0))]
+    for copy in copies:
+        copy.start()
     whole.wait()
     gx, me, gz = lax.axis_index("gx"), lax.axis_index("gy"), lax.axis_index("gz")
     stride = N_GZ * PER_DEV
@@ -185,14 +188,6 @@
         places.append(place)
         arrives.append((kind == 2) | (kind == 3))
     pays = (pay0, pay1, pay2)
-    u_copies = [pltpu.make_async_copy(f0.at[slots[k]], ubox.at[k], sems.at[k, 3]) for k in range(ROUNDS)]
-    copies = [
-        pltpu.make_async_copy(field.at[slots[k]], pays[k].at[pl.ds(f * BOX, BOX)], sems.at[k, f])
-        for k in range(ROUNDS)
-        for f, field in enumerate((f1, f2, f3))
-    ]
-    for copy in u_copies + copies:
-        copy.start()
     for q in range(PER_DEV):
         source = jnp.int32(0)
         for s in range(PER_DEV):
@@ -200,11 +195,12 @@
         for k in range(ROUNDS):
             source = source + _pick(arrives[k] & (places[k] == q), 4 + k, 0)
         plan[q] = source
-    for k in range(ROUNDS):
-        u_copies[k].wait()
-        halve(ubox.at[k], rows8.at[k], pays[k].at[pl.ds(3 * BOX, HALF)])
     for copy in copies:
         copy.wait()
+    for k in range(ROUNDS):
+        for f in range(3):
+            pays[k][f * BOX : (f + 1) * BOX, :] = boxes[f, slots[k]]
+        halve(boxes.at[3, slots[k]], rows8.at[k], pays[k].at[pl.ds(3 * BOX, HALF)])
 
 
 def halve(box, tmp, out):
@@ -235,9 +231,9 @@
             pltpu.SMEM((16,), jnp.int32),
             pltpu.SMEM((16,), jnp.int32),
             pltpu.SMEM((16,), jnp.int32),
-            pltpu.VMEM((ROUNDS, BOX, BOX * BOX), F32),
+            pltpu.VMEM((4, PER_DEV, BOX, BOX * BOX), F32),
             pltpu.VMEM((ROUNDS, 8, BOX, 128), F32),
-            pltpu.SemaphoreType.DMA((ROUNDS, 4)),
+            pltpu.SemaphoreType.DMA((4,)),
             pltpu.SemaphoreType.DMA,
         ],
         compiler_params=pltpu.CompilerParams(vmem_limit_bytes=60 * MIB),
@@ -629,7 +625,7 @@
             return carry
 
         out = half // 2
-        lax.fori_loop(1 + out, PAIRS - 1 - out, sweep, 0, unroll=2)
+        lax.fori_loop(1 + out, PAIRS - 1 - out, sweep, 0, unroll=3 if out else 4)
 
     def finish(j, carry):
         k = j + SIDE

time: 107 us -> 103 us (0.963)
  waiting for transfers between devices: 33.5 us -> 29.7 us
  starting transfers between devices: 46.8 us -> 49.7 us
  Pallas kernels: 23.2 us -> 20.8 us
    ppermute x2, starting transfers between devices: 2.74 us -> 9.76 us  [move(): return lax.ppermute(x, 'gy', pairs)]
    ppermute x5, starting transfers between devices: 20.7 us -> 17.7 us  [exchange(): lax.ppermute(odd, axis, pairs[1])]
    ppermute x5, waiting for transfers between devices: 8.49 us -> 6.16 us  [exchange(): lax.ppermute(odd, axis, pairs[1])]
    ppermute x2, waiting for transfers between devices: 25 us -> 23.6 us  [move(): return lax.ppermute(x, 'gy', pairs)]
    pallas_call x1, Pallas kernels: 3.85 us -> 2.53 us  [plan_and_pack(): pl.pallas_call(plan_kernel, out_shape=(*[jax.ShapeDtypeStruct((1,), jnp.i...]
    pallas_call x3, Pallas kernels: 13.1 us -> 12 us  [on_vmem(): pl.pallas_call(kernel, out_shape=out_shape, in_specs=[vmem] * len(args),...]
    ppermute x5, starting transfers between devices: 23.4 us -> 22.2 us  [exchange(): lax.ppermute(even, axis, pairs[0])]
where the time goes in v3:
time: 103 us
  starting transfers between devices  49.7 us (48%)
  waiting for transfers between devices  29.7 us (29%)
  Pallas kernels  20.8 us (20%)
  between operations  2.64 us (3%)
    ppermute x2, waiting for transfers between devices, move(): return lax.ppermute(x, 'gy', pairs)  23.6 us
    ppermute x5, starting transfers between devices, exchange(): lax.ppermute(even, axis, pairs[0])  22.2 us
    ppermute x5, starting transfers between devices, exchange(): lax.ppermute(odd, axis, pairs[1])  17.7 us
    pallas_call x3, Pallas kernels, on_vmem(): pl.pallas_call(kernel, out_shape=out_shape, in_specs=[vmem] * len(args),...  12 us
    ppermute x2, starting transfers between devices, move(): return lax.ppermute(x, 'gy', pairs)  9.76 us
    pallas_call x1, Pallas kernels, assemble(): pl.pallas_call(assemble_kernel, out_shape=(jax.ShapeDtypeStruct((7, HALF,...  6.23 us
    ppermute x5, waiting for transfers between devices, exchange(): lax.ppermute(odd, axis, pairs[1])  6.16 us
    pallas_call x1, Pallas kernels, plan_and_pack(): pl.pallas_call(plan_kernel, out_shape=(*[jax.ShapeDtypeStruct((1,), jnp.i...  2.53 us
  transfers between devices with their start and end apart: 12, of which 4 were waited for; matrix products, arithmetic and copies ran while one was open for 0% of the time, Pallas kernels for 1%

profile of v3, /device:TPU:1, one launch (start us, length us, event | category | flops | bytes accessed | tf_op | source)
XLA Modules:
  0.0 103.3 jit_solution(9437685124129383477)
XLA Ops:
  0.6 2.5 %plan.1 = (s32[1]{0:T(128)}, s32[1]{0:T(128)}, s32[1]{0:T(128)}, s32[4]{0:T(128)}, f32[112,1024]{1,0:T(8,128)S(1)}, /*index=5*/f32[112,1024]{1,0:T(8,128)S(1)}, f32[112,1024]{1,0:T(8,128)S(1)}) custom-call(s32[3,1024]{1,0:T(4,128)} %table.1, f32[4,32,1024]{2,1,0:T(8,128)} %f0.3, f32[4,32,1024]{2,1,0:T(8,128)} %f1.3, f32[4,32,1024]{2,1,0:T(8,128)} %f2.3, ...), custom_call_target="tpu_custom_call" | custom-call | tf_op jit(solution)/shard_map/plan/pallas_call | solution.py:223
  5.1 18.4 %conditional.4 = (f32[112,1024]{1,0:T(8,128)S(1)}) conditional(s32[]{:T(128)} %bitcast.1, f32[112,1024]{1,0:T(8,128)S(1)} %get-tuple-element.164, f32[112,1024]{1,0:T(8,128)S(1)} %get-tuple-element.164, f32[112,1024]{1,0:T(8,128)S(1)} %get-tuple-element.164, f32[112,1024]{1,0:T(8,128)S(1)} %get-tuple-element.164, ...), branch_computations={%region_22.0_spmd, %region_23.0_spmd, %region_24.0_spmd, %region_2... | conditional | bytes 2752560 | solution.py:258
  5.3 8.3 %collective-permute-start.34 = (f32[112,1024]{1,0:T(8,128)S(1)}, f32[112,1024]{1,0:T(8,128)S(1)}, u32[]{:S(2)}, u32[]{:S(2)}) collective-permute-start(f32[112,1024]{1,0:T(8,128)S(1)} %param.36), channel_id=1, source_target_pairs={{0,56},{8,48},{16,40},{24,32},{1,57},{9,49},{17,41},{25,33},{2,58}... | collective-permute-start | bytes 1376264 | tf_op jit(solution)/shard_map/cond/branch_14_fun/ppermute | solution.py:249
  13.7 9.8 %collective-permute-done.34 = f32[112,1024]{1,0:T(8,128)S(1)} collective-permute-done((f32[112,1024]{1,0:T(8,128)S(1)}, f32[112,1024]{1,0:T(8,128)S(1)}, u32[]{:S(2)}, u32[]{:S(2)}) %collective-permute-start.34) | collective-permute-done | bytes 458784 | tf_op jit(solution)/shard_map/cond/branch_14_fun/ppermute | solution.py:249
  23.5 0.0 copy-start
  23.5 0.0 copy-start.1
  23.5 0.0 copy-start.2
  23.6 15.3 %conditional.3 = (f32[112,1024]{1,0:T(8,128)S(1)}) conditional(s32[]{:T(128)} %bitcast, f32[112,1024]{1,0:T(8,128)S(1)} %get-tuple-element.162, f32[112,1024]{1,0:T(8,128)S(1)} %get-tuple-element.162, f32[112,1024]{1,0:T(8,128)S(1)} %get-tuple-element.162, f32[112,1024]{1,0:T(8,128)S(1)} %get-tuple-element.162, ...), branch_computations={%region_0.0_spmd, %region_1.0_spmd, %region_2.0_spmd, %region_3.0_... | conditional | bytes 2752560 | solution.py:258
  23.6 1.4 %collective-permute-start.15 = (f32[112,1024]{1,0:T(8,128)S(1)}, f32[112,1024]{1,0:T(8,128)S(1)}, u32[]{:S(2)}, u32[]{:S(2)}) collective-permute-start(f32[112,1024]{1,0:T(8,128)S(1)} %param.16), channel_id=1, source_target_pairs={{16,0},{24,8},{48,32},{56,40},{17,1},{25,9},{49,33},{57,41},{18,2}... | collective-permute-start | bytes 1376264 | tf_op jit(solution)/shard_map/cond/branch_16_fun/ppermute | solution.py:249
  25.1 13.7 %collective-permute-done.15 = f32[112,1024]{1,0:T(8,128)S(1)} collective-permute-done((f32[112,1024]{1,0:T(8,128)S(1)}, f32[112,1024]{1,0:T(8,128)S(1)}, u32[]{:S(2)}, u32[]{:S(2)}) %collective-permute-start.15) | collective-permute-done | bytes 458784 | tf_op jit(solution)/shard_map/cond/branch_16_fun/ppermute | solution.py:249
  38.9 6.2 %assemble.1 = (f32[7,16,32,128]{3,2,1,0:T(8,128)S(1)}, f32[14,32,128]{2,1,0:T(8,128)S(1)}, f32[14,32,128]{2,1,0:T(8,128)S(1)}, f32[56,8,128]{2,1,0:T(8,128)S(1)}...) custom-call(s32[4]{0:T(128)S(1)} %copy-done.4, f32[4,32,1024]{2,1,0:T(8,128)S(1)} %copy-done, ...), custom_call_target="tpu_custom_call" | custom-call | tf_op jit(solution)/shard_map/assemble/pallas_call | solution.py:435
  45.1 9.2 %collective-permute-start.63 = (f32[14,32,128]{2,1,0:T(8,128)S(1)}, f32[14,32,128]{2,1,0:T(8,128)S(1)}, u32[]{:S(2)}, u32[]{:S(2)}) collective-permute-start(f32[14,32,128]{2,1,0:T(8,128)S(1)} %get-tuple-element.168), channel_id=1, source_target_pairs={{0,64},{64,0},{128,192},{192,128},{1,65},{65,1},{129,193},{193,129... | collective-permute-start | bytes 688136 | tf_op jit(solution)/shard_map/ppermute | solution.py:688
  54.3 8.8 %collective-permute-start.64 = (f32[14,32,128]{2,1,0:T(8,128)S(1)}, f32[14,32,128]{2,1,0:T(8,128)S(1)}, u32[]{:S(2)}, u32[]{:S(2)}) collective-permute-start(f32[14,32,128]{2,1,0:T(8,128)S(1)} %get-tuple-element.169), channel_id=1, source_target_pairs={{64,128},{128,64},{192,0},{0,192},{65,129},{129,65},{193,1},{1,193... | collective-permute-start | bytes 688136 | tf_op jit(solution)/shard_map/ppermute | solution.py:688
  63.1 3.4 %collective-permute-done.64.x_odd = f32[14,32,128]{2,1,0:T(8,128)S(1)} collective-permute-done((f32[14,32,128]{2,1,0:T(8,128)S(1)}, f32[14,32,128]{2,1,0:T(8,128)S(1)}, u32[]{:S(2)}, u32[]{:S(2)}) %collective-permute-start.64) | collective-permute-done | bytes 229408 | tf_op jit(solution)/shard_map/ppermute | solution.py:688
  66.5 0.1 edge_y.1
  66.6 0.3 collective-permute-start.67
  66.8 0.1 collective-permute-start.68
  66.9 7.9 %collective-permute-start.69 = (f32[16,2,8,128]{3,2,1,0:T(8,128)S(1)}, f32[16,2,8,128]{3,2,1,0:T(8,128)S(1)}, u32[]{:S(2)}, u32[]{:S(2)}) collective-permute-start(f32[16,2,8,128]{3,2,1,0:T(8,128)S(1)} %get-tuple-element.181), channel_id=1, source_target_pairs={{0,1},{1,0},{2,3},{3,2},{4,5},{5,4},{6,7},{7,6},{8,9},{9,8},{10,11... | collective-permute-start | bytes 393224 | tf_op jit(solution)/shard_map/ppermute | solution.py:688
  74.9 1.7 %collective-permute-start.70 = (f32[16,2,8,128]{3,2,1,0:T(8,128)S(1)}, f32[16,2,8,128]{3,2,1,0:T(8,128)S(1)}, u32[]{:S(2)}, u32[]{:S(2)}) collective-permute-start(f32[16,2,8,128]{3,2,1,0:T(8,128)S(1)} %get-tuple-element.181), channel_id=1, source_target_pairs={{1,2},{2,1},{3,4},{4,3},{5,6},{6,5},{7,0},{0,7},{9,10},{10,9},{11,... | collective-permute-start | bytes 393224 | tf_op jit(solution)/shard_map/ppermute | solution.py:688
  76.6 1.2 %edge_z.1 = (f32[22,64,128]{2,1,0:T(8,128)S(1)}, f32[22,64,128]{2,1,0:T(8,128)S(1)}, f32[22,64,128]{2,1,0:T(8,128)S(1)}, f32[22,48,128]{2,1,0:T(8,128)S(1)}, f32...) custom-call(f32[7,16,32,128]{3,2,1,0:T(8,128)S(1)} %get-tuple-elemen, ...), custom_call_target="tpu_custom_call" | custom-call | tf_op jit(solution)/shard_map/edge_z/pallas_call | solution.py:647
  77.8 4.9 %collective-permute-start.71 = (f32[28,8,128]{2,1,0:T(8,128)S(1)}, f32[28,8,128]{2,1,0:T(8,128)S(1)}, u32[]{:S(2)}, u32[]{:S(2)}) collective-permute-start(f32[28,8,128]{2,1,0:T(8,128)S(1)} %get-tuple-element.182), channel_id=1, source_target_pairs={{0,1},{1,0},{2,3},{3,2},{4,5},{5,4},{6,7},{7,6},{8,9},{9,8},{10,11... | collective-permute-start | bytes 344072 | tf_op jit(solution)/shard_map/ppermute | solution.py:688
  82.7 7.1 %collective-permute-start.72 = (f32[28,8,128]{2,1,0:T(8,128)S(1)}, f32[28,8,128]{2,1,0:T(8,128)S(1)}, u32[]{:S(2)}, u32[]{:S(2)}) collective-permute-start(f32[28,8,128]{2,1,0:T(8,128)S(1)} %get-tuple-element.182), channel_id=1, source_target_pairs={{1,2},{2,1},{3,4},{4,3},{5,6},{6,5},{7,0},{0,7},{9,10},{10,9},{11,... | collective-permute-start | bytes 344072 | tf_op jit(solution)/shard_map/ppermute | solution.py:688
  89.8 2.8 %collective-permute-done.72.e_odd = f32[28,8,128]{2,1,0:T(8,128)S(1)} collective-permute-done((f32[28,8,128]{2,1,0:T(8,128)S(1)}, f32[28,8,128]{2,1,0:T(8,128)S(1)}, u32[]{:S(2)}, u32[]{:S(2)}) %collective-permute-start.72) | collective-permute-done | bytes 114720 | tf_op jit(solution)/shard_map/ppermute | solution.py:688
  92.6 10.7 %sweeps.1 = (f32[32,32,128]{2,1,0:T(8,128)}, f32[32,32,128]{2,1,0:T(8,128)}) custom-call(f32[22,64,128]{2,1,0:T(8,128)S(1)} %get-tuple-element.174.u1, f32[22,64,128]{2,1,0:T(8,128)S(1)} %get-tuple-element.175.b1, f32[22,64,128]{2,1,0:T(8,128)S(1)} %get-tuple-element.176.b0, f32[22,48,128]{2,1,0:T(8,128)S(1)} %get-tuple-element.177.f0, ...), custom_call_target="tpu_custom_call" | custom-call | tf_op jit(solution)/shard_map/sweeps/pallas_call | solution.py:647
  (20 shorter events, 0.2 us)
Async XLA Ops:
  5.3 18.2 %collective-permute-start.34 = (f32[112,1024]{1,0:T(8,128)S(1)}, f32[112,1024]{1,0:T(8,128)S(1)}, u32[]{:S(2)}, u32[]{:S(2)}) collective-permute-start(f32[112,1024]{1,0:T(8,128)S(1)} %param.36), channel_id=1, source_target_pairs={{0,56},{8,48},{16,40},{24,32},{1,57},{9,49},{17,41},{25,33},{2,58}... | collective-permute-start | bytes 1376264 | tf_op jit(solution)/shard_map/cond/branch_14_fun/ppermute | solution.py:249
  23.5 15.3 %copy-start = (f32[4,32,1024]{2,1,0:T(8,128)S(1)}, f32[4,32,1024]{2,1,0:T(8,128)}, u32[]{:S(2)}) copy-start(f32[4,32,1024]{2,1,0:T(8,128)} %f0.3) | copy-start | bytes 1572868
  23.5 15.3 %copy-start.1 = (f32[4,32,1024]{2,1,0:T(8,128)S(1)}, f32[4,32,1024]{2,1,0:T(8,128)}, u32[]{:S(2)}) copy-start(f32[4,32,1024]{2,1,0:T(8,128)} %f1.3) | copy-start | bytes 1572868
  23.5 15.3 %copy-start.2 = (f32[4,32,1024]{2,1,0:T(8,128)S(1)}, f32[4,32,1024]{2,1,0:T(8,128)}, u32[]{:S(2)}) copy-start(f32[4,32,1024]{2,1,0:T(8,128)} %f2.3) | copy-start | bytes 1572868
  23.6 15.3 %copy-start.3 = (f32[4,32,1024]{2,1,0:T(8,128)S(1)}, f32[4,32,1024]{2,1,0:T(8,128)}, u32[]{:S(2)}) copy-start(f32[4,32,1024]{2,1,0:T(8,128)} %f3.3) | copy-start | bytes 1572868
  23.6 15.3 %copy-start.4 = (s32[4]{0:T(128)S(1)}, s32[4]{0:T(128)}, u32[]{:S(2)}) copy-start(s32[4]{0:T(128)} %get-tuple-element.160.plan) | copy-start | bytes 52
  23.6 15.2 %collective-permute-start.15 = (f32[112,1024]{1,0:T(8,128)S(1)}, f32[112,1024]{1,0:T(8,128)S(1)}, u32[]{:S(2)}, u32[]{:S(2)}) collective-permute-start(f32[112,1024]{1,0:T(8,128)S(1)} %param.16), channel_id=1, source_target_pairs={{16,0},{24,8},{48,32},{56,40},{17,1},{25,9},{49,33},{57,41},{18,2}... | collective-permute-start | bytes 1376264 | tf_op jit(solution)/shard_map/cond/branch_16_fun/ppermute | solution.py:249
  45.1 17.9 %collective-permute-start.63 = (f32[14,32,128]{2,1,0:T(8,128)S(1)}, f32[14,32,128]{2,1,0:T(8,128)S(1)}, u32[]{:S(2)}, u32[]{:S(2)}) collective-permute-start(f32[14,32,128]{2,1,0:T(8,128)S(1)} %get-tuple-element.168), channel_id=1, source_target_pairs={{0,64},{64,0},{128,192},{192,128},{1,65},{65,1},{129,193},{193,129... | collective-permute-start | bytes 688136 | tf_op jit(solution)/shard_map/ppermute | solution.py:688
  54.3 12.2 %collective-permute-start.64 = (f32[14,32,128]{2,1,0:T(8,128)S(1)}, f32[14,32,128]{2,1,0:T(8,128)S(1)}, u32[]{:S(2)}, u32[]{:S(2)}) collective-permute-start(f32[14,32,128]{2,1,0:T(8,128)S(1)} %get-tuple-element.169), channel_id=1, source_target_pairs={{64,128},{128,64},{192,0},{0,192},{65,129},{129,65},{193,1},{1,193... | collective-permute-start | bytes 688136 | tf_op jit(solution)/shard_map/ppermute | solution.py:688
  63.1 11.8 %collective-permute-start.65 = (f32[56,8,128]{2,1,0:T(8,128)S(1)}, f32[56,8,128]{2,1,0:T(8,128)S(1)}, u32[]{:S(2)}, u32[]{:S(2)}) collective-permute-start(f32[56,8,128]{2,1,0:T(8,128)S(1)} %get-tuple-element.170), channel_id=1, source_target_pairs={{0,8},{8,0},{16,24},{24,16},{32,40},{40,32},{48,56},{56,48},{1,9},... | collective-permute-start | bytes 688136 | tf_op jit(solution)/shard_map/ppermute | solution.py:688
  63.1 13.5 %collective-permute-start.66 = (f32[56,8,128]{2,1,0:T(8,128)S(1)}, f32[56,8,128]{2,1,0:T(8,128)S(1)}, u32[]{:S(2)}, u32[]{:S(2)}) collective-permute-start(f32[56,8,128]{2,1,0:T(8,128)S(1)} %get-tuple-element.171), channel_id=1, source_target_pairs={{8,16},{16,8},{24,32},{32,24},{40,48},{48,40},{56,0},{0,56},{9,17}... | collective-permute-start | bytes 688136 | tf_op jit(solution)/shard_map/ppermute | solution.py:688
  66.6 10.0 %collective-permute-start.67 = (f32[14,8,128]{2,1,0:T(8,128)S(1)}, f32[14,8,128]{2,1,0:T(8,128)S(1)}, u32[]{:S(2)}, u32[]{:S(2)}) collective-permute-start(f32[14,8,128]{2,1,0:T(8,128)S(1)} %get-tuple-element.172), channel_id=1, source_target_pairs={{0,8},{8,0},{16,24},{24,16},{32,40},{40,32},{48,56},{56,48},{1,9},... | collective-permute-start | bytes 172040 | tf_op jit(solution)/shard_map/ppermute | solution.py:688
  66.8 9.7 %collective-permute-start.68 = (f32[14,8,128]{2,1,0:T(8,128)S(1)}, f32[14,8,128]{2,1,0:T(8,128)S(1)}, u32[]{:S(2)}, u32[]{:S(2)}) collective-permute-start(f32[14,8,128]{2,1,0:T(8,128)S(1)} %get-tuple-element.173), channel_id=1, source_target_pairs={{8,16},{16,8},{24,32},{32,24},{40,48},{48,40},{56,0},{0,56},{9,17}... | collective-permute-start | bytes 172040 | tf_op jit(solution)/shard_map/ppermute | solution.py:688
  66.9 22.9 %collective-permute-start.69 = (f32[16,2,8,128]{3,2,1,0:T(8,128)S(1)}, f32[16,2,8,128]{3,2,1,0:T(8,128)S(1)}, u32[]{:S(2)}, u32[]{:S(2)}) collective-permute-start(f32[16,2,8,128]{3,2,1,0:T(8,128)S(1)} %get-tuple-element.181), channel_id=1, source_target_pairs={{0,1},{1,0},{2,3},{3,2},{4,5},{5,4},{6,7},{7,6},{8,9},{9,8},{10,11... | collective-permute-start | bytes 393224 | tf_op jit(solution)/shard_map/ppermute | solution.py:688
  74.9 15.0 %collective-permute-start.70 = (f32[16,2,8,128]{3,2,1,0:T(8,128)S(1)}, f32[16,2,8,128]{3,2,1,0:T(8,128)S(1)}, u32[]{:S(2)}, u32[]{:S(2)}) collective-permute-start(f32[16,2,8,128]{3,2,1,0:T(8,128)S(1)} %get-tuple-element.181), channel_id=1, source_target_pairs={{1,2},{2,1},{3,4},{4,3},{5,6},{6,5},{7,0},{0,7},{9,10},{10,9},{11,... | collective-permute-start | bytes 393224 | tf_op jit(solution)/shard_map/ppermute | solution.py:688
  77.8 12.0 %collective-permute-start.71 = (f32[28,8,128]{2,1,0:T(8,128)S(1)}, f32[28,8,128]{2,1,0:T(8,128)S(1)}, u32[]{:S(2)}, u32[]{:S(2)}) collective-permute-start(f32[28,8,128]{2,1,0:T(8,128)S(1)} %get-tuple-element.182), channel_id=1, source_target_pairs={{0,1},{1,0},{2,3},{3,2},{4,5},{5,4},{6,7},{7,6},{8,9},{9,8},{10,11... | collective-permute-start | bytes 344072 | tf_op jit(solution)/shard_map/ppermute | solution.py:688
  82.7 9.9 %collective-permute-start.72 = (f32[28,8,128]{2,1,0:T(8,128)S(1)}, f32[28,8,128]{2,1,0:T(8,128)S(1)}, u32[]{:S(2)}, u32[]{:S(2)}) collective-permute-start(f32[28,8,128]{2,1,0:T(8,128)S(1)} %get-tuple-element.182), channel_id=1, source_target_pairs={{1,2},{2,1},{3,4},{4,3},{5,6},{6,5},{7,0},{0,7},{9,10},{10,9},{11,... | collective-permute-start | bytes 344072 | tf_op jit(solution)/shard_map/ppermute | solution.py:688

commit v4 on v3

--- a/solution.py
+++ b/solution.py
@@ -563,7 +563,7 @@
         return carry
 
     um1[...] = u1[...]
-    lax.fori_loop(0, HALF, unpack_pair, 0, unroll=2)
+    lax.fori_loop(0, HALF, unpack_pair, 0, unroll=4)
     for i, k in enumerate(EDGES):
         for v in range(3):
             unpack(k, e_even[3 * i + v], e_odd[3 * i + v], (2 * v, 2 * v + 1))
@@ -602,7 +602,7 @@
                         dg[c, k - 1, rows, :] = diag
         return carry
 
-    lax.fori_loop(1, PAIRS - 1, coefs, 0, unroll=2)
+    lax.fori_loop(1, PAIRS - 1, coefs, 0, unroll=4)
 
     def update(c, k, t, spans):
         rows = slice(t * 8, 8 + t * 8)
@@ -625,7 +625,7 @@
             return carry
 
         out = half // 2
-        lax.fori_loop(1 + out, PAIRS - 1 - out, sweep, 0, unroll=3 if out else 4)
+        lax.fori_loop(1 + out, PAIRS - 1 - out, sweep, 0, unroll=6 if out else 5)
 
     def finish(j, carry):
         k = j + SIDE
@@ -639,7 +639,7 @@
                 ref[2 * j + 1, ys, :] = jnp.where(is_odd, v0, v1)
         return carry
 
-    lax.fori_loop(0, HALF, finish, 0, unroll=2)
+    lax.fori_loop(0, HALF, finish, 0, unroll=4)
 
 
 def on_vmem(kernel, out_shape, scratch, name, limit, *args):

time: 103 us -> 104 us (level); the launches traced: 103 us -> 102 us
  starting transfers between devices: 49.7 us -> 43.1 us
  waiting for transfers between devices: 29.7 us -> 36.2 us
  Pallas kernels: 20.8 us -> 19.6 us
    ppermute x2 -> x3, waiting for transfers between devices: 23.6 us -> 31.7 us  [move(): return lax.ppermute(x, 'gy', pairs)]
    ppermute x5, starting transfers between devices: 17.7 us -> 11.4 us  [exchange(): lax.ppermute(odd, axis, pairs[1])]
    ppermute x5, waiting for transfers between devices: 6.16 us -> 4.51 us  [exchange(): lax.ppermute(odd, axis, pairs[1])]
    pallas_call x3, Pallas kernels: 12 us -> 10.9 us  [on_vmem(): pl.pallas_call(kernel, out_shape=out_shape, in_specs=[vmem] * len(args),...]
    ppermute x2 -> x3, starting transfers between devices: 9.76 us -> 8.97 us  [move(): return lax.ppermute(x, 'gy', pairs)]
  transfers between devices with their start and end apart: 12 -> 13, of which waited for: 4 -> 5; matrix products, arithmetic and copies ran while one was open for 0% -> 0% of each run, Pallas kernels for 1% -> 1%
where the time goes in v4:
time: 104 us; the launch traced here: 102 us
  starting transfers between devices  43.1 us (41%)
  waiting for transfers between devices  36.2 us (35%)
  Pallas kernels  19.6 us (19%)
  between operations  2.64 us (3%)
    ppermute x3, waiting for transfers between devices, move(): return lax.ppermute(x, 'gy', pairs)  31.7 us
    ppermute x5, starting transfers between devices, exchange(): lax.ppermute(even, axis, pairs[0])  22.7 us
    ppermute x5, starting transfers between devices, exchange(): lax.ppermute(odd, axis, pairs[1])  11.4 us
    pallas_call x3, Pallas kernels, on_vmem(): pl.pallas_call(kernel, out_shape=out_shape, in_specs=[vmem] * len(args),...  10.9 us
    ppermute x3, starting transfers between devices, move(): return lax.ppermute(x, 'gy', pairs)  8.97 us
    pallas_call x1, Pallas kernels, assemble(): pl.pallas_call(assemble_kernel, out_shape=(jax.ShapeDtypeStruct((7, HALF,...  6.14 us
    ppermute x5, waiting for transfers between devices, exchange(): lax.ppermute(odd, axis, pairs[1])  4.51 us
    pallas_call x1, Pallas kernels, plan_and_pack(): pl.pallas_call(plan_kernel, out_shape=(*[jax.ShapeDtypeStruct((1,), jnp.i...  2.53 us
  transfers between devices with their start and end apart: 13, of which 5 were waited for; matrix products, arithmetic and copies ran while one was open for 0% of the time, Pallas kernels for 1%

profile of v4, /device:TPU:1, one launch (start us, length us, event | category | flops | bytes accessed | tf_op | source)
XLA Modules:
  0.0 102.0 jit_solution(16201094338355118323)
XLA Ops:
  0.6 2.5 %plan.1 = (s32[1]{0:T(128)}, s32[1]{0:T(128)}, s32[1]{0:T(128)}, s32[4]{0:T(128)}, f32[112,1024]{1,0:T(8,128)S(1)}, /*index=5*/f32[112,1024]{1,0:T(8,128)S(1)}, f32[112,1024]{1,0:T(8,128)S(1)}) custom-call(s32[3,1024]{1,0:T(4,128)} %table.1, f32[4,32,1024]{2,1,0:T(8,128)} %f0.3, f32[4,32,1024]{2,1,0:T(8,128)} %f1.3, f32[4,32,1024]{2,1,0:T(8,128)} %f2.3, ...), custom_call_target="tpu_custom_call" | custom-call | tf_op jit(solution)/shard_map/plan/pallas_call | solution.py:223
  5.0 21.6 %conditional.5 = (f32[112,1024]{1,0:T(8,128)S(1)}) conditional(s32[]{:T(128)} %bitcast.2, f32[112,1024]{1,0:T(8,128)S(1)} %get-tuple-element.166, f32[112,1024]{1,0:T(8,128)S(1)} %get-tuple-element.166, f32[112,1024]{1,0:T(8,128)S(1)} %get-tuple-element.166, f32[112,1024]{1,0:T(8,128)S(1)} %get-tuple-element.166, ...), branch_computations={%region_44.0_spmd, %region_45.0_spmd, %region_46.0_spmd, %region_4... | conditional | bytes 2752560 | solution.py:258
  5.1 7.1 %collective-permute-start.51 = (f32[112,1024]{1,0:T(8,128)S(1)}, f32[112,1024]{1,0:T(8,128)S(1)}, u32[]{:S(2)}, u32[]{:S(2)}) collective-permute-start(f32[112,1024]{1,0:T(8,128)S(1)} %param.54), channel_id=1, source_target_pairs={{0,24},{8,16},{32,56},{40,48},{1,25},{9,17},{33,57},{41,49},{2,26}... | collective-permute-start | bytes 1376264 | tf_op jit(solution)/shard_map/cond/branch_10_fun/ppermute | solution.py:249
  12.2 14.4 %collective-permute-done.51 = f32[112,1024]{1,0:T(8,128)S(1)} collective-permute-done((f32[112,1024]{1,0:T(8,128)S(1)}, f32[112,1024]{1,0:T(8,128)S(1)}, u32[]{:S(2)}, u32[]{:S(2)}) %collective-permute-start.51) | collective-permute-done | bytes 458784 | tf_op jit(solution)/shard_map/cond/branch_10_fun/ppermute | solution.py:249
  26.6 8.9 %conditional.4 = (f32[112,1024]{1,0:T(8,128)S(1)}) conditional(s32[]{:T(128)} %bitcast.1, f32[112,1024]{1,0:T(8,128)S(1)} %get-tuple-element.164, f32[112,1024]{1,0:T(8,128)S(1)} %get-tuple-element.164, f32[112,1024]{1,0:T(8,128)S(1)} %get-tuple-element.164, f32[112,1024]{1,0:T(8,128)S(1)} %get-tuple-element.164, ...), branch_computations={%region_22.0_spmd, %region_23.0_spmd, %region_24.0_spmd, %region_2... | conditional | bytes 2752560 | solution.py:258
  26.7 0.4 collective-permute-start.27
  27.1 8.2 %collective-permute-done.27 = f32[112,1024]{1,0:T(8,128)S(1)} collective-permute-done((f32[112,1024]{1,0:T(8,128)S(1)}, f32[112,1024]{1,0:T(8,128)S(1)}, u32[]{:S(2)}, u32[]{:S(2)}) %collective-permute-start.27) | collective-permute-done | bytes 458784 | tf_op jit(solution)/shard_map/cond/branch_7_fun/ppermute | solution.py:249
  35.5 0.0 copy-start.1
  35.5 0.0 copy-start.2
  35.6 10.6 %conditional.3 = (f32[112,1024]{1,0:T(8,128)S(1)}) conditional(s32[]{:T(128)} %bitcast, f32[112,1024]{1,0:T(8,128)S(1)} %get-tuple-element.162, f32[112,1024]{1,0:T(8,128)S(1)} %get-tuple-element.162, f32[112,1024]{1,0:T(8,128)S(1)} %get-tuple-element.162, f32[112,1024]{1,0:T(8,128)S(1)} %get-tuple-element.162, ...), branch_computations={%region_0.0_spmd, %region_1.0_spmd, %region_2.0_spmd, %region_3.0_... | conditional | bytes 2752560 | solution.py:258
  35.6 1.4 %collective-permute-start.15 = (f32[112,1024]{1,0:T(8,128)S(1)}, f32[112,1024]{1,0:T(8,128)S(1)}, u32[]{:S(2)}, u32[]{:S(2)}) collective-permute-start(f32[112,1024]{1,0:T(8,128)S(1)} %param.16), channel_id=1, source_target_pairs={{16,0},{24,8},{48,32},{56,40},{17,1},{25,9},{49,33},{57,41},{18,2}... | collective-permute-start | bytes 1376264 | tf_op jit(solution)/shard_map/cond/branch_16_fun/ppermute | solution.py:249
  37.1 9.1 %collective-permute-done.15 = f32[112,1024]{1,0:T(8,128)S(1)} collective-permute-done((f32[112,1024]{1,0:T(8,128)S(1)}, f32[112,1024]{1,0:T(8,128)S(1)}, u32[]{:S(2)}, u32[]{:S(2)}) %collective-permute-start.15) | collective-permute-done | bytes 458784 | tf_op jit(solution)/shard_map/cond/branch_16_fun/ppermute | solution.py:249
  46.3 6.1 %assemble.1 = (f32[7,16,32,128]{3,2,1,0:T(8,128)S(1)}, f32[14,32,128]{2,1,0:T(8,128)S(1)}, f32[14,32,128]{2,1,0:T(8,128)S(1)}, f32[56,8,128]{2,1,0:T(8,128)S(1)}...) custom-call(s32[4]{0:T(128)S(1)} %copy-done.4, f32[4,32,1024]{2,1,0:T(8,128)S(1)} %copy-done, ...), custom_call_target="tpu_custom_call" | custom-call | tf_op jit(solution)/shard_map/assemble/pallas_call | solution.py:435
  52.4 4.8 %collective-permute-start.63 = (f32[14,32,128]{2,1,0:T(8,128)S(1)}, f32[14,32,128]{2,1,0:T(8,128)S(1)}, u32[]{:S(2)}, u32[]{:S(2)}) collective-permute-start(f32[14,32,128]{2,1,0:T(8,128)S(1)} %get-tuple-element.168), channel_id=1, source_target_pairs={{0,64},{64,0},{128,192},{192,128},{1,65},{65,1},{129,193},{193,129... | collective-permute-start | bytes 688136 | tf_op jit(solution)/shard_map/ppermute | solution.py:688
  57.2 8.0 %collective-permute-start.66 = (f32[56,8,128]{2,1,0:T(8,128)S(1)}, f32[56,8,128]{2,1,0:T(8,128)S(1)}, u32[]{:S(2)}, u32[]{:S(2)}) collective-permute-start(f32[56,8,128]{2,1,0:T(8,128)S(1)} %get-tuple-element.171), channel_id=1, source_target_pairs={{8,16},{16,8},{24,32},{32,24},{40,48},{48,40},{56,0},{0,56},{9,17}... | collective-permute-start | bytes 688136 | tf_op jit(solution)/shard_map/ppermute | solution.py:688
  65.2 0.1 edge_y.1
  65.4 0.3 collective-permute-start.67
  65.6 3.4 %collective-permute-start.68 = (f32[14,8,128]{2,1,0:T(8,128)S(1)}, f32[14,8,128]{2,1,0:T(8,128)S(1)}, u32[]{:S(2)}, u32[]{:S(2)}) collective-permute-start(f32[14,8,128]{2,1,0:T(8,128)S(1)} %get-tuple-element.173), channel_id=1, source_target_pairs={{8,16},{16,8},{24,32},{32,24},{40,48},{48,40},{56,0},{0,56},{9,17}... | collective-permute-start | bytes 172040 | tf_op jit(solution)/shard_map/ppermute | solution.py:688
  69.0 15.4 %collective-permute-start.69 = (f32[16,2,8,128]{3,2,1,0:T(8,128)S(1)}, f32[16,2,8,128]{3,2,1,0:T(8,128)S(1)}, u32[]{:S(2)}, u32[]{:S(2)}) collective-permute-start(f32[16,2,8,128]{3,2,1,0:T(8,128)S(1)} %get-tuple-element.181), channel_id=1, source_target_pairs={{0,1},{1,0},{2,3},{3,2},{4,5},{5,4},{6,7},{7,6},{8,9},{9,8},{10,11... | collective-permute-start | bytes 393224 | tf_op jit(solution)/shard_map/ppermute | solution.py:688
  84.4 1.2 %edge_z.1 = (f32[22,64,128]{2,1,0:T(8,128)S(1)}, f32[22,64,128]{2,1,0:T(8,128)S(1)}, f32[22,64,128]{2,1,0:T(8,128)S(1)}, f32[22,48,128]{2,1,0:T(8,128)S(1)}, f32...) custom-call(f32[7,16,32,128]{3,2,1,0:T(8,128)S(1)} %get-tuple-elemen, ...), custom_call_target="tpu_custom_call" | custom-call | tf_op jit(solution)/shard_map/edge_z/pallas_call | solution.py:647
  85.7 2.3 %collective-permute-start.71 = (f32[28,8,128]{2,1,0:T(8,128)S(1)}, f32[28,8,128]{2,1,0:T(8,128)S(1)}, u32[]{:S(2)}, u32[]{:S(2)}) collective-permute-start(f32[28,8,128]{2,1,0:T(8,128)S(1)} %get-tuple-element.182), channel_id=1, source_target_pairs={{0,1},{1,0},{2,3},{3,2},{4,5},{5,4},{6,7},{7,6},{8,9},{9,8},{10,11... | collective-permute-start | bytes 344072 | tf_op jit(solution)/shard_map/ppermute | solution.py:688
  87.9 1.2 %collective-permute-done.70.z_odd = f32[16,2,8,128]{3,2,1,0:T(8,128)S(1)} collective-permute-done((f32[16,2,8,128]{3,2,1,0:T(8,128)S(1)}, f32[16,2,8,128]{3,2,1,0:T(8,128)S(1)}, u32[]{:S(2)}, u32[]{:S(2)}) %collective-permute-start.70) | collective-permute-done | bytes 131104 | tf_op jit(solution)/shard_map/ppermute | solution.py:688
  89.1 3.4 %collective-permute-done.72.e_odd = f32[28,8,128]{2,1,0:T(8,128)S(1)} collective-permute-done((f32[28,8,128]{2,1,0:T(8,128)S(1)}, f32[28,8,128]{2,1,0:T(8,128)S(1)}, u32[]{:S(2)}, u32[]{:S(2)}) %collective-permute-start.72) | collective-permute-done | bytes 114720 | tf_op jit(solution)/shard_map/ppermute | solution.py:688
  92.5 9.6 %sweeps.1 = (f32[32,32,128]{2,1,0:T(8,128)}, f32[32,32,128]{2,1,0:T(8,128)}) custom-call(f32[22,64,128]{2,1,0:T(8,128)S(1)} %get-tuple-element.174.u1, f32[22,64,128]{2,1,0:T(8,128)S(1)} %get-tuple-element.175.b1, f32[22,64,128]{2,1,0:T(8,128)S(1)} %get-tuple-element.176.b0, f32[22,48,128]{2,1,0:T(8,128)S(1)} %get-tuple-element.177.f0, ...), custom_call_target="tpu_custom_call" | custom-call | tf_op jit(solution)/shard_map/sweeps/pallas_call | solution.py:647
  (23 shorter events, 0.1 us)
Async XLA Ops:
  5.1 21.5 %collective-permute-start.51 = (f32[112,1024]{1,0:T(8,128)S(1)}, f32[112,1024]{1,0:T(8,128)S(1)}, u32[]{:S(2)}, u32[]{:S(2)}) collective-permute-start(f32[112,1024]{1,0:T(8,128)S(1)} %param.54), channel_id=1, source_target_pairs={{0,24},{8,16},{32,56},{40,48},{1,25},{9,17},{33,57},{41,49},{2,26}... | collective-permute-start | bytes 1376264 | tf_op jit(solution)/shard_map/cond/branch_10_fun/ppermute | solution.py:249
  26.7 8.6 %collective-permute-start.27 = (f32[112,1024]{1,0:T(8,128)S(1)}, f32[112,1024]{1,0:T(8,128)S(1)}, u32[]{:S(2)}, u32[]{:S(2)}) collective-permute-start(f32[112,1024]{1,0:T(8,128)S(1)} %param.29), channel_id=1, source_target_pairs={{0,56},{8,48},{16,40},{24,32},{32,24},{40,16},{48,8},{56,0},{1,57}... | collective-permute-start | bytes 1376264 | tf_op jit(solution)/shard_map/cond/branch_7_fun/ppermute | solution.py:249
  35.5 10.7 %copy-start = (f32[4,32,1024]{2,1,0:T(8,128)S(1)}, f32[4,32,1024]{2,1,0:T(8,128)}, u32[]{:S(2)}) copy-start(f32[4,32,1024]{2,1,0:T(8,128)} %f0.3) | copy-start | bytes 1572868
  35.5 10.7 %copy-start.1 = (f32[4,32,1024]{2,1,0:T(8,128)S(1)}, f32[4,32,1024]{2,1,0:T(8,128)}, u32[]{:S(2)}) copy-start(f32[4,32,1024]{2,1,0:T(8,128)} %f1.3) | copy-start | bytes 1572868
  35.5 10.7 %copy-start.2 = (f32[4,32,1024]{2,1,0:T(8,128)S(1)}, f32[4,32,1024]{2,1,0:T(8,128)}, u32[]{:S(2)}) copy-start(f32[4,32,1024]{2,1,0:T(8,128)} %f2.3) | copy-start | bytes 1572868
  35.6 10.7 %copy-start.3 = (f32[4,32,1024]{2,1,0:T(8,128)S(1)}, f32[4,32,1024]{2,1,0:T(8,128)}, u32[]{:S(2)}) copy-start(f32[4,32,1024]{2,1,0:T(8,128)} %f3.3) | copy-start | bytes 1572868
  35.6 10.7 %copy-start.4 = (s32[4]{0:T(128)S(1)}, s32[4]{0:T(128)}, u32[]{:S(2)}) copy-start(s32[4]{0:T(128)} %get-tuple-element.160.plan) | copy-start | bytes 52
  35.6 10.5 %collective-permute-start.15 = (f32[112,1024]{1,0:T(8,128)S(1)}, f32[112,1024]{1,0:T(8,128)S(1)}, u32[]{:S(2)}, u32[]{:S(2)}) collective-permute-start(f32[112,1024]{1,0:T(8,128)S(1)} %param.16), channel_id=1, source_target_pairs={{16,0},{24,8},{48,32},{56,40},{17,1},{25,9},{49,33},{57,41},{18,2}... | collective-permute-start | bytes 1376264 | tf_op jit(solution)/shard_map/cond/branch_16_fun/ppermute | solution.py:249
  52.4 12.8 %collective-permute-start.63 = (f32[14,32,128]{2,1,0:T(8,128)S(1)}, f32[14,32,128]{2,1,0:T(8,128)S(1)}, u32[]{:S(2)}, u32[]{:S(2)}) collective-permute-start(f32[14,32,128]{2,1,0:T(8,128)S(1)} %get-tuple-element.168), channel_id=1, source_target_pairs={{0,64},{64,0},{128,192},{192,128},{1,65},{65,1},{129,193},{193,129... | collective-permute-start | bytes 688136 | tf_op jit(solution)/shard_map/ppermute | solution.py:688
  57.2 8.1 %collective-permute-start.64 = (f32[14,32,128]{2,1,0:T(8,128)S(1)}, f32[14,32,128]{2,1,0:T(8,128)S(1)}, u32[]{:S(2)}, u32[]{:S(2)}) collective-permute-start(f32[14,32,128]{2,1,0:T(8,128)S(1)} %get-tuple-element.169), channel_id=1, source_target_pairs={{64,128},{128,64},{192,0},{0,192},{65,129},{129,65},{193,1},{1,193... | collective-permute-start | bytes 688136 | tf_op jit(solution)/shard_map/ppermute | solution.py:688
  57.2 27.2 %collective-permute-start.65 = (f32[56,8,128]{2,1,0:T(8,128)S(1)}, f32[56,8,128]{2,1,0:T(8,128)S(1)}, u32[]{:S(2)}, u32[]{:S(2)}) collective-permute-start(f32[56,8,128]{2,1,0:T(8,128)S(1)} %get-tuple-element.170), channel_id=1, source_target_pairs={{0,8},{8,0},{16,24},{24,16},{32,40},{40,32},{48,56},{56,48},{1,9},... | collective-permute-start | bytes 688136 | tf_op jit(solution)/shard_map/ppermute | solution.py:688
  57.2 27.2 %collective-permute-start.66 = (f32[56,8,128]{2,1,0:T(8,128)S(1)}, f32[56,8,128]{2,1,0:T(8,128)S(1)}, u32[]{:S(2)}, u32[]{:S(2)}) collective-permute-start(f32[56,8,128]{2,1,0:T(8,128)S(1)} %get-tuple-element.171), channel_id=1, source_target_pairs={{8,16},{16,8},{24,32},{32,24},{40,48},{48,40},{56,0},{0,56},{9,17}... | collective-permute-start | bytes 688136 | tf_op jit(solution)/shard_map/ppermute | solution.py:688
  65.4 19.1 %collective-permute-start.67 = (f32[14,8,128]{2,1,0:T(8,128)S(1)}, f32[14,8,128]{2,1,0:T(8,128)S(1)}, u32[]{:S(2)}, u32[]{:S(2)}) collective-permute-start(f32[14,8,128]{2,1,0:T(8,128)S(1)} %get-tuple-element.172), channel_id=1, source_target_pairs={{0,8},{8,0},{16,24},{24,16},{32,40},{40,32},{48,56},{56,48},{1,9},... | collective-permute-start | bytes 172040 | tf_op jit(solution)/shard_map/ppermute | solution.py:688
  65.6 18.8 %collective-permute-start.68 = (f32[14,8,128]{2,1,0:T(8,128)S(1)}, f32[14,8,128]{2,1,0:T(8,128)S(1)}, u32[]{:S(2)}, u32[]{:S(2)}) collective-permute-start(f32[14,8,128]{2,1,0:T(8,128)S(1)} %get-tuple-element.173), channel_id=1, source_target_pairs={{8,16},{16,8},{24,32},{32,24},{40,48},{48,40},{56,0},{0,56},{9,17}... | collective-permute-start | bytes 172040 | tf_op jit(solution)/shard_map/ppermute | solution.py:688
  69.0 18.9 %collective-permute-start.69 = (f32[16,2,8,128]{3,2,1,0:T(8,128)S(1)}, f32[16,2,8,128]{3,2,1,0:T(8,128)S(1)}, u32[]{:S(2)}, u32[]{:S(2)}) collective-permute-start(f32[16,2,8,128]{3,2,1,0:T(8,128)S(1)} %get-tuple-element.181), channel_id=1, source_target_pairs={{0,1},{1,0},{2,3},{3,2},{4,5},{5,4},{6,7},{7,6},{8,9},{9,8},{10,11... | collective-permute-start | bytes 393224 | tf_op jit(solution)/shard_map/ppermute | solution.py:688
  84.4 4.7 %collective-permute-start.70 = (f32[16,2,8,128]{3,2,1,0:T(8,128)S(1)}, f32[16,2,8,128]{3,2,1,0:T(8,128)S(1)}, u32[]{:S(2)}, u32[]{:S(2)}) collective-permute-start(f32[16,2,8,128]{3,2,1,0:T(8,128)S(1)} %get-tuple-element.181), channel_id=1, source_target_pairs={{1,2},{2,1},{3,4},{4,3},{5,6},{6,5},{7,0},{0,7},{9,10},{10,9},{11,... | collective-permute-start | bytes 393224 | tf_op jit(solution)/shard_map/ppermute | solution.py:688
  85.7 3.4 %collective-permute-start.71 = (f32[28,8,128]{2,1,0:T(8,128)S(1)}, f32[28,8,128]{2,1,0:T(8,128)S(1)}, u32[]{:S(2)}, u32[]{:S(2)}) collective-permute-start(f32[28,8,128]{2,1,0:T(8,128)S(1)} %get-tuple-element.182), channel_id=1, source_target_pairs={{0,1},{1,0},{2,3},{3,2},{4,5},{5,4},{6,7},{7,6},{8,9},{9,8},{10,11... | collective-permute-start | bytes 344072 | tf_op jit(solution)/shard_map/ppermute | solution.py:688
  87.9 4.5 %collective-permute-start.72 = (f32[28,8,128]{2,1,0:T(8,128)S(1)}, f32[28,8,128]{2,1,0:T(8,128)S(1)}, u32[]{:S(2)}, u32[]{:S(2)}) collective-permute-start(f32[28,8,128]{2,1,0:T(8,128)S(1)} %get-tuple-element.182), channel_id=1, source_target_pairs={{1,2},{2,1},{3,4},{4,3},{5,6},{6,5},{7,0},{0,7},{9,10},{10,9},{11,... | collective-permute-start | bytes 344072 | tf_op jit(solution)/shard_map/ppermute | solution.py:688

commit v5 on v4

--- a/solution.py
+++ b/solution.py
@@ -128,9 +128,9 @@
             for i, j in flows:
                 d = (j - i) & 7
                 ahead = _pick(d <= 4, d, 0)
-                back = _pick(d <= 4, 0, 8 - d)
-                load[0] = load[0] + jnp.where(((link - i) & 7) < ahead, unit, 0)
-                load[1] = load[1] + jnp.where(((i - link) & 7) < back, unit, 0)
+                back = _pick(d < 4, 0, 8 - d)
+                load[0] = load[0] + jnp.where(((link - i) & 7) < ahead, unit * _pick(d == 4, 1, 2), 0)
+                load[1] = load[1] + jnp.where(((i - link) & 7) < back, unit * _pick(d == 4, 1, 2), 0)
     cost = jnp.zeros((8, 128), F32)
     for r in range(ROUNDS):
         busiest = jnp.maximum(*[(lax.shift_right_logical(v, 8 * r) & 255).astype(F32) for v in load])

time: 104 us -> 108 us (1.038)
  the two profiles are of different devices: /device:TPU:1 before, /device:TPU:17 now
where the time goes in v5:
time: 108 us
  starting transfers between devices  53.1 us (49%)
  waiting for transfers between devices  32.6 us (30%)
  Pallas kernels  19.6 us (18%)
  between operations  2.63 us (2%)
    ppermute x5, starting transfers between devices, exchange(): lax.ppermute(even, axis, pairs[0])  28.8 us
    ppermute x3, waiting for transfers between devices, move(): return lax.ppermute(x, 'gy', pairs)  27.5 us
    ppermute x3, starting transfers between devices, move(): return lax.ppermute(x, 'gy', pairs)  18.7 us
    pallas_call x3, Pallas kernels, on_vmem(): pl.pallas_call(kernel, out_shape=out_shape, in_specs=[vmem] * len(args),...  10.9 us
    pallas_call x1, Pallas kernels, assemble(): pl.pallas_call(assemble_kernel, out_shape=(jax.ShapeDtypeStruct((7, HALF,...  6.14 us
    ppermute x5, starting transfers between devices, exchange(): lax.ppermute(odd, axis, pairs[1])  5.66 us
    ppermute x5, waiting for transfers between devices, exchange(): lax.ppermute(odd, axis, pairs[1])  4.12 us
    pallas_call x1, Pallas kernels, plan_and_pack(): pl.pallas_call(plan_kernel, out_shape=(*[jax.ShapeDtypeStruct((1,), jnp.i...  2.56 us
  transfers between devices with their start and end apart: 13, of which 6 were waited for; matrix products, arithmetic and copies ran while one was open for 0% of the time, Pallas kernels for 1%

profile of v5, /device:TPU:17, one launch (start us, length us, event | category | flops | bytes accessed | tf_op | source)
XLA Modules:
  0.0 108.4 jit_solution(5149425953727056434)
XLA Ops:
  0.6 2.6 %plan.1 = (s32[1]{0:T(128)}, s32[1]{0:T(128)}, s32[1]{0:T(128)}, s32[4]{0:T(128)}, f32[112,1024]{1,0:T(8,128)S(1)}, /*index=5*/f32[112,1024]{1,0:T(8,128)S(1)}, f32[112,1024]{1,0:T(8,128)S(1)}) custom-call(s32[3,1024]{1,0:T(4,128)} %table.1, f32[4,32,1024]{2,1,0:T(8,128)} %f0.3, f32[4,32,1024]{2,1,0:T(8,128)} %f1.3, f32[4,32,1024]{2,1,0:T(8,128)} %f2.3, ...), custom_call_target="tpu_custom_call" | custom-call | tf_op jit(solution)/shard_map/plan/pallas_call | solution.py:223
  5.0 13.2 %conditional.5 = (f32[112,1024]{1,0:T(8,128)S(1)}) conditional(s32[]{:T(128)} %bitcast.2, f32[112,1024]{1,0:T(8,128)S(1)} %get-tuple-element.166, f32[112,1024]{1,0:T(8,128)S(1)} %get-tuple-element.166, f32[112,1024]{1,0:T(8,128)S(1)} %get-tuple-element.166, f32[112,1024]{1,0:T(8,128)S(1)} %get-tuple-element.166, ...), branch_computations={%region_44.0_spmd, %region_45.0_spmd, %region_46.0_spmd, %region_4... | conditional | bytes 2752560 | solution.py:258
  5.1 1.3 %collective-permute-start.57 = (f32[112,1024]{1,0:T(8,128)S(1)}, f32[112,1024]{1,0:T(8,128)S(1)}, u32[]{:S(2)}, u32[]{:S(2)}) collective-permute-start(f32[112,1024]{1,0:T(8,128)S(1)} %param.60), channel_id=1, source_target_pairs={{16,0},{24,8},{48,32},{56,40},{17,1},{25,9},{49,33},{57,41},{18,2}... | collective-permute-start | bytes 1376264 | tf_op jit(solution)/shard_map/cond/branch_16_fun/ppermute | solution.py:249
  6.4 11.8 %collective-permute-done.57 = f32[112,1024]{1,0:T(8,128)S(1)} collective-permute-done((f32[112,1024]{1,0:T(8,128)S(1)}, f32[112,1024]{1,0:T(8,128)S(1)}, u32[]{:S(2)}, u32[]{:S(2)}) %collective-permute-start.57) | collective-permute-done | bytes 458784 | tf_op jit(solution)/shard_map/cond/branch_16_fun/ppermute | solution.py:249
  18.2 11.4 %conditional.4 = (f32[112,1024]{1,0:T(8,128)S(1)}) conditional(s32[]{:T(128)} %bitcast.1, f32[112,1024]{1,0:T(8,128)S(1)} %get-tuple-element.164, f32[112,1024]{1,0:T(8,128)S(1)} %get-tuple-element.164, f32[112,1024]{1,0:T(8,128)S(1)} %get-tuple-element.164, f32[112,1024]{1,0:T(8,128)S(1)} %get-tuple-element.164, ...), branch_computations={%region_22.0_spmd, %region_23.0_spmd, %region_24.0_spmd, %region_2... | conditional | bytes 2752560 | solution.py:258
  18.3 5.7 %collective-permute-start.28 = (f32[112,1024]{1,0:T(8,128)S(1)}, f32[112,1024]{1,0:T(8,128)S(1)}, u32[]{:S(2)}, u32[]{:S(2)}) collective-permute-start(f32[112,1024]{1,0:T(8,128)S(1)} %param.30), channel_id=1, source_target_pairs={{0,8},{16,24},{32,40},{48,56},{1,9},{17,25},{33,41},{49,57},{2,10}... | collective-permute-start | bytes 1376264 | tf_op jit(solution)/shard_map/cond/branch_8_fun/ppermute | solution.py:249
  24.0 5.4 %collective-permute-done.28 = f32[112,1024]{1,0:T(8,128)S(1)} collective-permute-done((f32[112,1024]{1,0:T(8,128)S(1)}, f32[112,1024]{1,0:T(8,128)S(1)}, u32[]{:S(2)}, u32[]{:S(2)}) %collective-permute-start.28) | collective-permute-done | bytes 458784 | tf_op jit(solution)/shard_map/cond/branch_8_fun/ppermute | solution.py:249
  29.7 22.1 %conditional.3 = (f32[112,1024]{1,0:T(8,128)S(1)}) conditional(s32[]{:T(128)} %bitcast, f32[112,1024]{1,0:T(8,128)S(1)} %get-tuple-element.162, f32[112,1024]{1,0:T(8,128)S(1)} %get-tuple-element.162, f32[112,1024]{1,0:T(8,128)S(1)} %get-tuple-element.162, f32[112,1024]{1,0:T(8,128)S(1)} %get-tuple-element.162, ...), branch_computations={%region_0.0_spmd, %region_1.0_spmd, %region_2.0_spmd, %region_3.0_... | conditional | bytes 2752560 | solution.py:258
  29.7 11.6 %collective-permute-start.4 = (f32[112,1024]{1,0:T(8,128)S(1)}, f32[112,1024]{1,0:T(8,128)S(1)}, u32[]{:S(2)}, u32[]{:S(2)}) collective-permute-start(f32[112,1024]{1,0:T(8,128)S(1)} %param.5), channel_id=1, source_target_pairs={{0,40},{8,32},{16,56},{24,48},{32,8},{40,0},{48,24},{56,16},{1,41}... | collective-permute-start | bytes 1376264 | tf_op jit(solution)/shard_map/cond/branch_5_fun/ppermute | solution.py:249
  41.3 10.3 %collective-permute-done.4 = f32[112,1024]{1,0:T(8,128)S(1)} collective-permute-done((f32[112,1024]{1,0:T(8,128)S(1)}, f32[112,1024]{1,0:T(8,128)S(1)}, u32[]{:S(2)}, u32[]{:S(2)}) %collective-permute-start.4) | collective-permute-done | bytes 458784 | tf_op jit(solution)/shard_map/cond/branch_5_fun/ppermute | solution.py:249
  51.8 6.1 %assemble.1 = (f32[7,16,32,128]{3,2,1,0:T(8,128)S(1)}, f32[14,32,128]{2,1,0:T(8,128)S(1)}, f32[14,32,128]{2,1,0:T(8,128)S(1)}, f32[56,8,128]{2,1,0:T(8,128)S(1)}...) custom-call(s32[4]{0:T(128)S(1)} %copy-done.4, f32[4,32,1024]{2,1,0:T(8,128)S(1)} %copy-done, ...), custom_call_target="tpu_custom_call" | custom-call | tf_op jit(solution)/shard_map/assemble/pallas_call | solution.py:435
  57.9 2.6 %collective-permute-start.63 = (f32[14,32,128]{2,1,0:T(8,128)S(1)}, f32[14,32,128]{2,1,0:T(8,128)S(1)}, u32[]{:S(2)}, u32[]{:S(2)}) collective-permute-start(f32[14,32,128]{2,1,0:T(8,128)S(1)} %get-tuple-element.168), channel_id=1, source_target_pairs={{0,64},{64,0},{128,192},{192,128},{1,65},{65,1},{129,193},{193,129... | collective-permute-start | bytes 688136 | tf_op jit(solution)/shard_map/ppermute | solution.py:688
  60.6 1.6 %collective-permute-start.64 = (f32[14,32,128]{2,1,0:T(8,128)S(1)}, f32[14,32,128]{2,1,0:T(8,128)S(1)}, u32[]{:S(2)}, u32[]{:S(2)}) collective-permute-start(f32[14,32,128]{2,1,0:T(8,128)S(1)} %get-tuple-element.169), channel_id=1, source_target_pairs={{64,128},{128,64},{192,0},{0,192},{65,129},{129,65},{193,1},{1,193... | collective-permute-start | bytes 688136 | tf_op jit(solution)/shard_map/ppermute | solution.py:688
  62.2 0.7 collective-permute-start.65
  62.9 3.2 %collective-permute-start.66 = (f32[56,8,128]{2,1,0:T(8,128)S(1)}, f32[56,8,128]{2,1,0:T(8,128)S(1)}, u32[]{:S(2)}, u32[]{:S(2)}) collective-permute-start(f32[56,8,128]{2,1,0:T(8,128)S(1)} %get-tuple-element.171), channel_id=1, source_target_pairs={{8,16},{16,8},{24,32},{32,24},{40,48},{48,40},{56,0},{0,56},{9,17}... | collective-permute-start | bytes 688136 | tf_op jit(solution)/shard_map/ppermute | solution.py:688
  66.1 0.9 collective-permute-done.64.x_odd
  67.0 2.1 %collective-permute-start.67 = (f32[14,8,128]{2,1,0:T(8,128)S(1)}, f32[14,8,128]{2,1,0:T(8,128)S(1)}, u32[]{:S(2)}, u32[]{:S(2)}) collective-permute-start(f32[14,8,128]{2,1,0:T(8,128)S(1)} %get-tuple-element.172), channel_id=1, source_target_pairs={{0,8},{8,0},{16,24},{24,16},{32,40},{40,32},{48,56},{56,48},{1,9},... | collective-permute-start | bytes 172040 | tf_op jit(solution)/shard_map/ppermute | solution.py:688
  69.1 0.8 collective-permute-start.68
  69.9 18.1 %collective-permute-start.69 = (f32[16,2,8,128]{3,2,1,0:T(8,128)S(1)}, f32[16,2,8,128]{3,2,1,0:T(8,128)S(1)}, u32[]{:S(2)}, u32[]{:S(2)}) collective-permute-start(f32[16,2,8,128]{3,2,1,0:T(8,128)S(1)} %get-tuple-element.181), channel_id=1, source_target_pairs={{0,1},{1,0},{2,3},{3,2},{4,5},{5,4},{6,7},{7,6},{8,9},{9,8},{10,11... | collective-permute-start | bytes 393224 | tf_op jit(solution)/shard_map/ppermute | solution.py:688
  88.1 1.2 %edge_z.1 = (f32[22,64,128]{2,1,0:T(8,128)S(1)}, f32[22,64,128]{2,1,0:T(8,128)S(1)}, f32[22,64,128]{2,1,0:T(8,128)S(1)}, f32[22,48,128]{2,1,0:T(8,128)S(1)}, f32...) custom-call(f32[7,16,32,128]{3,2,1,0:T(8,128)S(1)} %get-tuple-elemen, ...), custom_call_target="tpu_custom_call" | custom-call | tf_op jit(solution)/shard_map/edge_z/pallas_call | solution.py:647
  89.3 5.3 %collective-permute-start.71 = (f32[28,8,128]{2,1,0:T(8,128)S(1)}, f32[28,8,128]{2,1,0:T(8,128)S(1)}, u32[]{:S(2)}, u32[]{:S(2)}) collective-permute-start(f32[28,8,128]{2,1,0:T(8,128)S(1)} %get-tuple-element.182), channel_id=1, source_target_pairs={{0,1},{1,0},{2,3},{3,2},{4,5},{5,4},{6,7},{7,6},{8,9},{9,8},{10,11... | collective-permute-start | bytes 344072 | tf_op jit(solution)/shard_map/ppermute | solution.py:688
  94.6 1.0 collective-permute-done.71.e_even
  95.6 3.3 %collective-permute-done.72.e_odd = f32[28,8,128]{2,1,0:T(8,128)S(1)} collective-permute-done((f32[28,8,128]{2,1,0:T(8,128)S(1)}, f32[28,8,128]{2,1,0:T(8,128)S(1)}, u32[]{:S(2)}, u32[]{:S(2)}) %collective-permute-start.72) | collective-permute-done | bytes 114720 | tf_op jit(solution)/shard_map/ppermute | solution.py:688
  98.8 9.6 %sweeps.1 = (f32[32,32,128]{2,1,0:T(8,128)}, f32[32,32,128]{2,1,0:T(8,128)}) custom-call(f32[22,64,128]{2,1,0:T(8,128)S(1)} %get-tuple-element.174.u1, f32[22,64,128]{2,1,0:T(8,128)S(1)} %get-tuple-element.175.b1, f32[22,64,128]{2,1,0:T(8,128)S(1)} %get-tuple-element.176.b0, f32[22,48,128]{2,1,0:T(8,128)S(1)} %get-tuple-element.177.f0, ...), custom_call_target="tpu_custom_call" | custom-call | tf_op jit(solution)/shard_map/sweeps/pallas_call | solution.py:647
  (23 shorter events, 0.2 us)
Async XLA Ops:
  5.1 13.1 %collective-permute-start.57 = (f32[112,1024]{1,0:T(8,128)S(1)}, f32[112,1024]{1,0:T(8,128)S(1)}, u32[]{:S(2)}, u32[]{:S(2)}) collective-permute-start(f32[112,1024]{1,0:T(8,128)S(1)} %param.60), channel_id=1, source_target_pairs={{16,0},{24,8},{48,32},{56,40},{17,1},{25,9},{49,33},{57,41},{18,2}... | collective-permute-start | bytes 1376264 | tf_op jit(solution)/shard_map/cond/branch_16_fun/ppermute | solution.py:249
  18.3 11.1 %collective-permute-start.28 = (f32[112,1024]{1,0:T(8,128)S(1)}, f32[112,1024]{1,0:T(8,128)S(1)}, u32[]{:S(2)}, u32[]{:S(2)}) collective-permute-start(f32[112,1024]{1,0:T(8,128)S(1)} %param.30), channel_id=1, source_target_pairs={{0,8},{16,24},{32,40},{48,56},{1,9},{17,25},{33,41},{49,57},{2,10}... | collective-permute-start | bytes 1376264 | tf_op jit(solution)/shard_map/cond/branch_8_fun/ppermute | solution.py:249
  29.6 22.1 %copy-start = (f32[4,32,1024]{2,1,0:T(8,128)S(1)}, f32[4,32,1024]{2,1,0:T(8,128)}, u32[]{:S(2)}) copy-start(f32[4,32,1024]{2,1,0:T(8,128)} %f0.3) | copy-start | bytes 1572868
  29.6 22.1 %copy-start.1 = (f32[4,32,1024]{2,1,0:T(8,128)S(1)}, f32[4,32,1024]{2,1,0:T(8,128)}, u32[]{:S(2)}) copy-start(f32[4,32,1024]{2,1,0:T(8,128)} %f1.3) | copy-start | bytes 1572868
  29.6 22.1 %copy-start.2 = (f32[4,32,1024]{2,1,0:T(8,128)S(1)}, f32[4,32,1024]{2,1,0:T(8,128)}, u32[]{:S(2)}) copy-start(f32[4,32,1024]{2,1,0:T(8,128)} %f2.3) | copy-start | bytes 1572868
  29.7 22.1 %copy-start.3 = (f32[4,32,1024]{2,1,0:T(8,128)S(1)}, f32[4,32,1024]{2,1,0:T(8,128)}, u32[]{:S(2)}) copy-start(f32[4,32,1024]{2,1,0:T(8,128)} %f3.3) | copy-start | bytes 1572868
  29.7 22.1 %copy-start.4 = (s32[4]{0:T(128)S(1)}, s32[4]{0:T(128)}, u32[]{:S(2)}) copy-start(s32[4]{0:T(128)} %get-tuple-element.160.plan) | copy-start | bytes 52
  29.7 22.0 %collective-permute-start.4 = (f32[112,1024]{1,0:T(8,128)S(1)}, f32[112,1024]{1,0:T(8,128)S(1)}, u32[]{:S(2)}, u32[]{:S(2)}) collective-permute-start(f32[112,1024]{1,0:T(8,128)S(1)} %param.5), channel_id=1, source_target_pairs={{0,40},{8,32},{16,56},{24,48},{32,8},{40,0},{48,24},{56,16},{1,41}... | collective-permute-start | bytes 1376264 | tf_op jit(solution)/shard_map/cond/branch_5_fun/ppermute | solution.py:249
  57.9 8.1 %collective-permute-start.63 = (f32[14,32,128]{2,1,0:T(8,128)S(1)}, f32[14,32,128]{2,1,0:T(8,128)S(1)}, u32[]{:S(2)}, u32[]{:S(2)}) collective-permute-start(f32[14,32,128]{2,1,0:T(8,128)S(1)} %get-tuple-element.168), channel_id=1, source_target_pairs={{0,64},{64,0},{128,192},{192,128},{1,65},{65,1},{129,193},{193,129... | collective-permute-start | bytes 688136 | tf_op jit(solution)/shard_map/ppermute | solution.py:688
  60.6 6.4 %collective-permute-start.64 = (f32[14,32,128]{2,1,0:T(8,128)S(1)}, f32[14,32,128]{2,1,0:T(8,128)S(1)}, u32[]{:S(2)}, u32[]{:S(2)}) collective-permute-start(f32[14,32,128]{2,1,0:T(8,128)S(1)} %get-tuple-element.169), channel_id=1, source_target_pairs={{64,128},{128,64},{192,0},{0,192},{65,129},{129,65},{193,1},{1,193... | collective-permute-start | bytes 688136 | tf_op jit(solution)/shard_map/ppermute | solution.py:688
  62.2 25.8 %collective-permute-start.65 = (f32[56,8,128]{2,1,0:T(8,128)S(1)}, f32[56,8,128]{2,1,0:T(8,128)S(1)}, u32[]{:S(2)}, u32[]{:S(2)}) collective-permute-start(f32[56,8,128]{2,1,0:T(8,128)S(1)} %get-tuple-element.170), channel_id=1, source_target_pairs={{0,8},{8,0},{16,24},{24,16},{32,40},{40,32},{48,56},{56,48},{1,9},... | collective-permute-start | bytes 688136 | tf_op jit(solution)/shard_map/ppermute | solution.py:688
  62.9 25.2 %collective-permute-start.66 = (f32[56,8,128]{2,1,0:T(8,128)S(1)}, f32[56,8,128]{2,1,0:T(8,128)S(1)}, u32[]{:S(2)}, u32[]{:S(2)}) collective-permute-start(f32[56,8,128]{2,1,0:T(8,128)S(1)} %get-tuple-element.171), channel_id=1, source_target_pairs={{8,16},{16,8},{24,32},{32,24},{40,48},{48,40},{56,0},{0,56},{9,17}... | collective-permute-start | bytes 688136 | tf_op jit(solution)/shard_map/ppermute | solution.py:688
  67.0 21.0 %collective-permute-start.67 = (f32[14,8,128]{2,1,0:T(8,128)S(1)}, f32[14,8,128]{2,1,0:T(8,128)S(1)}, u32[]{:S(2)}, u32[]{:S(2)}) collective-permute-start(f32[14,8,128]{2,1,0:T(8,128)S(1)} %get-tuple-element.172), channel_id=1, source_target_pairs={{0,8},{8,0},{16,24},{24,16},{32,40},{40,32},{48,56},{56,48},{1,9},... | collective-permute-start | bytes 172040 | tf_op jit(solution)/shard_map/ppermute | solution.py:688
  69.1 18.9 %collective-permute-start.68 = (f32[14,8,128]{2,1,0:T(8,128)S(1)}, f32[14,8,128]{2,1,0:T(8,128)S(1)}, u32[]{:S(2)}, u32[]{:S(2)}) collective-permute-start(f32[14,8,128]{2,1,0:T(8,128)S(1)} %get-tuple-element.173), channel_id=1, source_target_pairs={{8,16},{16,8},{24,32},{32,24},{40,48},{48,40},{56,0},{0,56},{9,17}... | collective-permute-start | bytes 172040 | tf_op jit(solution)/shard_map/ppermute | solution.py:688
  69.9 24.7 %collective-permute-start.69 = (f32[16,2,8,128]{3,2,1,0:T(8,128)S(1)}, f32[16,2,8,128]{3,2,1,0:T(8,128)S(1)}, u32[]{:S(2)}, u32[]{:S(2)}) collective-permute-start(f32[16,2,8,128]{3,2,1,0:T(8,128)S(1)} %get-tuple-element.181), channel_id=1, source_target_pairs={{0,1},{1,0},{2,3},{3,2},{4,5},{5,4},{6,7},{7,6},{8,9},{9,8},{10,11... | collective-permute-start | bytes 393224 | tf_op jit(solution)/shard_map/ppermute | solution.py:688
  88.0 6.6 %collective-permute-start.70 = (f32[16,2,8,128]{3,2,1,0:T(8,128)S(1)}, f32[16,2,8,128]{3,2,1,0:T(8,128)S(1)}, u32[]{:S(2)}, u32[]{:S(2)}) collective-permute-start(f32[16,2,8,128]{3,2,1,0:T(8,128)S(1)} %get-tuple-element.181), channel_id=1, source_target_pairs={{1,2},{2,1},{3,4},{4,3},{5,6},{6,5},{7,0},{0,7},{9,10},{10,9},{11,... | collective-permute-start | bytes 393224 | tf_op jit(solution)/shard_map/ppermute | solution.py:688
  89.3 6.3 %collective-permute-start.71 = (f32[28,8,128]{2,1,0:T(8,128)S(1)}, f32[28,8,128]{2,1,0:T(8,128)S(1)}, u32[]{:S(2)}, u32[]{:S(2)}) collective-permute-start(f32[28,8,128]{2,1,0:T(8,128)S(1)} %get-tuple-element.182), channel_id=1, source_target_pairs={{0,1},{1,0},{2,3},{3,2},{4,5},{5,4},{6,7},{7,6},{8,9},{9,8},{10,11... | collective-permute-start | bytes 344072 | tf_op jit(solution)/shard_map/ppermute | solution.py:688
  94.6 4.2 %collective-permute-start.72 = (f32[28,8,128]{2,1,0:T(8,128)S(1)}, f32[28,8,128]{2,1,0:T(8,128)S(1)}, u32[]{:S(2)}, u32[]{:S(2)}) collective-permute-start(f32[28,8,128]{2,1,0:T(8,128)S(1)} %get-tuple-element.182), channel_id=1, source_target_pairs={{1,2},{2,1},{3,4},{4,3},{5,6},{6,5},{7,0},{0,7},{9,10},{10,9},{11,... | collective-permute-start | bytes 344072 | tf_op jit(solution)/shard_map/ppermute | solution.py:688
